TPU v7x, 32 devices: a whole 2x2x4 slice. The times are simulated.
32 devices in a mesh: doc: 8 (over y, x, core), seq: 4 (over z).
Axes of the slice: x: 2, y: 2, z: 4, core: 2. Of those that a mesh axis runs over, the one named last changes fastest.
Arguments:
- inputs: bfloat16 [16, 1024, 768], P('doc', 'seq'), may hold values from -6 to 6
- attn_gain: float32 [768], replicated, may hold values from 0.5 to 1.5
- qkv_weight: bfloat16 [768, 2304], replicated, may hold values from -0.25 to 0.25
- attn_out_weight: bfloat16 [768, 768], replicated, may hold values from -2 to 2
- mlp_gain: float32 [768], replicated, may hold values from 0.5 to 1.5
- mlp_in_weight: bfloat16 [768, 2304], replicated, may hold values from -0.21875 to 0.21875
- mlp_out_weight: bfloat16 [1152, 768], replicated, may hold values from -0.1875 to 0.1875
- cotangent: bfloat16 [16, 1024, 768], P('doc', 'seq'), may hold values from -6 to 6
Outputs:
- output: bfloat16 [16, 1024, 768], P('doc', 'seq')
- input_grad: bfloat16 [16, 1024, 768], P('doc', 'seq')
- attn_gain_grad: float32 [768], replicated
- qkv_weight_grad: float32 [768, 2304], replicated
- attn_out_weight_grad: float32 [768, 768], replicated
- mlp_gain_grad: float32 [768], replicated
- mlp_in_weight_grad: float32 [768, 2304], replicated
- mlp_out_weight_grad: float32 [1152, 768], replicated
All inputs are finite; a program needn't handle non-finite values.
Results may differ from a plain program's by a relative error of at most 0.015.
Values may be sent and summed in bfloat16 or wider, within the bound.
A program may use at most 128 MiB of HBM per device.

v0:
```python
import jax
import jax.numpy as jnp
from jax import lax
from jax.sharding import PartitionSpec as P

HEAD_DIM = 64


ROPE_THETA = 160000.0
NORM_EPSILON = 1e-05


def norm_rows(values, scale_gain):
    row_mean = jnp.mean(values, axis=-1, keepdims=True)
    centered = values - row_mean
    variance = jnp.mean(centered * centered, axis=-1, keepdims=True)
    return centered * lax.rsqrt(variance + NORM_EPSILON) * scale_gain


def rotary_tables(positions, head_width):
    half_width = head_width // 2
    frequency = ROPE_THETA ** (-(jnp.arange(half_width, dtype=jnp.float32) * 2.0) / head_width)
    angles = positions.astype(jnp.float32)[:, None] * frequency[None, :]
    angles = jnp.concatenate([angles, angles], axis=-1)
    return (jnp.cos(angles)[:, None, :], jnp.sin(angles)[:, None, :])


def rotate(values, cosine_table, sine_table):
    half_width = values.shape[-1] // 2
    turned = jnp.concatenate([-values[..., half_width:], values[..., :half_width]], axis=-1)
    return values * cosine_table + turned * sine_table


def rotate_back(gradient, cosine_table, sine_table):
    half_width = gradient.shape[-1] // 2
    sined = gradient * sine_table
    turned = jnp.concatenate([sined[..., half_width:], -sined[..., :half_width]], axis=-1)
    return gradient * cosine_table + turned


def gelu_product(gate_up):
    half_width = gate_up.shape[-1] // 2
    return jax.nn.gelu(gate_up[..., :half_width], approximate=False) * gate_up[..., half_width:]


def split_heads(columns):
    return columns.reshape(columns.shape[0], columns.shape[1] // HEAD_DIM, HEAD_DIM)


def attend_forward(queries, key_rows, value_rows):
    length, features = queries.shape
    scores = (
        jnp.einsum(
            "qhd,khd->hqk",
            split_heads(queries),
            split_heads(key_rows),
            preferred_element_type=jnp.float32,
        )
        * 0.125
    )
    row_max = jnp.max(scores, axis=-1, keepdims=True)
    exp_scores = jnp.exp(scores - row_max)
    row_total = jnp.sum(exp_scores, axis=-1, keepdims=True)
    softmax_low = (exp_scores / row_total).astype(jnp.bfloat16)
    mixed_rows = jnp.einsum(
        "hqk,khd->qhd", softmax_low, split_heads(value_rows), preferred_element_type=jnp.float32
    )
    return (
        mixed_rows.reshape(length, features).astype(jnp.bfloat16),
        (row_max + jnp.log(row_total))[..., 0],
    )


def attend_backward(queries, key_rows, value_rows, grad_mixed, log_total, cosine_table, sine_table):
    length, features = queries.shape
    query_heads = split_heads(queries)
    key_heads = split_heads(key_rows)
    value_heads = split_heads(value_rows)
    grad_heads = split_heads(grad_mixed)
    scores = (
        jnp.einsum("qhd,khd->hqk", query_heads, key_heads, preferred_element_type=jnp.float32)
        * 0.125
    )
    softmax_out = jnp.exp(scores - log_total[..., None])
    grad_soft = jnp.einsum(
        "qhd,khd->hqk", grad_heads, value_heads, preferred_element_type=jnp.float32
    )
    row_inner = jnp.sum(softmax_out * grad_soft, axis=-1, keepdims=True)
    grad_scores = (softmax_out * (grad_soft - row_inner)).astype(jnp.bfloat16)
    grad_query = (
        jnp.einsum("hqk,khd->qhd", grad_scores, key_heads, preferred_element_type=jnp.float32)
        * 0.125
    )
    grad_key = (
        jnp.einsum("hqk,qhd->khd", grad_scores, query_heads, preferred_element_type=jnp.float32)
        * 0.125
    )
    grad_value = jnp.einsum(
        "hqk,qhd->khd",
        softmax_out.astype(jnp.bfloat16),
        grad_heads,
        preferred_element_type=jnp.float32,
    )
    grad_query = (
        rotate_back(grad_query, cosine_table, sine_table)
        .reshape(length, features)
        .astype(jnp.bfloat16)
    )
    grad_key = (
        rotate_back(grad_key, cosine_table, sine_table)
        .reshape(length, features)
        .astype(jnp.bfloat16)
    )
    return (grad_query, grad_key, grad_value.reshape(length, features).astype(jnp.bfloat16))


def per_device(
    inputs,
    attn_gain,
    qkv_weight,
    attn_out_weight,
    mlp_gain,
    mlp_in_weight,
    mlp_out_weight,
    cotangent,
):
    doc_count, row_count, features = inputs.shape
    token_count = doc_count * row_count
    length = row_count * lax.axis_size("seq")
    flat_in = inputs.reshape(token_count, features).astype(jnp.float32)
    normed = norm_rows(flat_in, attn_gain).astype(jnp.bfloat16)
    projected = jnp.dot(normed, qkv_weight, preferred_element_type=jnp.float32)
    projected = projected.reshape(doc_count, row_count, 3 * features)
    local_cos, local_sin = rotary_tables(
        lax.axis_index("seq") * row_count + jnp.arange(row_count, dtype=jnp.int32), HEAD_DIM
    )

    def turned_low(columns):
        shaped = columns.reshape(doc_count, row_count, features // HEAD_DIM, HEAD_DIM)
        return (
            rotate(shaped, local_cos, local_sin)
            .reshape(doc_count, row_count, features)
            .astype(jnp.bfloat16)
        )

    queries = turned_low(projected[..., :features])
    key_rows = turned_low(projected[..., features : 2 * features])
    value_rows = projected[..., 2 * features :].astype(jnp.bfloat16)
    head_queries, head_keys, head_values = (
        lax.all_to_all(queries, "seq", split_axis=2, concat_axis=1, tiled=True),
        lax.all_to_all(key_rows, "seq", split_axis=2, concat_axis=1, tiled=True),
        lax.all_to_all(value_rows, "seq", split_axis=2, concat_axis=1, tiled=True),
    )
    mixed_heads, log_total = lax.map(
        lambda bundle: attend_forward(*bundle), (head_queries, head_keys, head_values)
    )
    attended = lax.all_to_all(mixed_heads, "seq", split_axis=1, concat_axis=2, tiled=True).reshape(
        token_count, features
    )
    hidden_res = flat_in + jnp.dot(attended, attn_out_weight, preferred_element_type=jnp.float32)
    normed_two = norm_rows(hidden_res, mlp_gain).astype(jnp.bfloat16)
    gate_up = jnp.dot(normed_two, mlp_in_weight, preferred_element_type=jnp.float32)
    inner_act, inner_pull = jax.vjp(gelu_product, gate_up)
    inner_act = inner_act.astype(jnp.bfloat16)
    result = hidden_res + jnp.dot(inner_act, mlp_out_weight, preferred_element_type=jnp.float32)
    output = result.astype(jnp.bfloat16).reshape(doc_count, row_count, features)
    upstream = cotangent.reshape(token_count, features)
    grad_mlp_out = jnp.einsum("tf,td->fd", inner_act, upstream, preferred_element_type=jnp.float32)
    grad_inner = jnp.einsum(
        "td,fd->tf", upstream, mlp_out_weight, preferred_element_type=jnp.float32
    )
    grad_gate_up = inner_pull(grad_inner)[0].astype(jnp.bfloat16)
    grad_mlp_in = jnp.einsum(
        "td,tf->df", normed_two, grad_gate_up, preferred_element_type=jnp.float32
    )
    grad_normed_two = jnp.einsum(
        "tf,df->td", grad_gate_up, mlp_in_weight, preferred_element_type=jnp.float32
    )
    _, second_pull = jax.vjp(norm_rows, hidden_res, mlp_gain)
    grad_hidden, grad_mlp_gain = second_pull(grad_normed_two)
    grad_hidden = grad_hidden + upstream.astype(jnp.float32)
    grad_branch = grad_hidden.astype(jnp.bfloat16)
    grad_attn_out = jnp.einsum(
        "td,te->de", attended, grad_branch, preferred_element_type=jnp.float32
    )
    grad_attended = jnp.einsum(
        "te,de->td", grad_branch, attn_out_weight, preferred_element_type=jnp.float32
    )
    grad_attended = grad_attended.astype(jnp.bfloat16).reshape(doc_count, row_count, features)
    grad_mixed = lax.all_to_all(grad_attended, "seq", split_axis=2, concat_axis=1, tiled=True)
    full_cos, full_sin = rotary_tables(jnp.arange(length, dtype=jnp.int32), HEAD_DIM)
    grad_head_q, grad_head_k, grad_head_v = lax.map(
        lambda bundle: attend_backward(*bundle, full_cos, full_sin),
        (head_queries, head_keys, head_values, grad_mixed, log_total),
    )
    grad_tok_q, grad_tok_k, grad_tok_v = (
        lax.all_to_all(grad_head_q, "seq", split_axis=1, concat_axis=2, tiled=True),
        lax.all_to_all(grad_head_k, "seq", split_axis=1, concat_axis=2, tiled=True),
        lax.all_to_all(grad_head_v, "seq", split_axis=1, concat_axis=2, tiled=True),
    )
    grad_tok_q = grad_tok_q.reshape(token_count, features)
    grad_tok_k = grad_tok_k.reshape(token_count, features)
    grad_tok_v = grad_tok_v.reshape(token_count, features)
    grad_qkv = jnp.concatenate(
        [
            jnp.einsum("td,te->de", normed, grad_tok_q, preferred_element_type=jnp.float32),
            jnp.einsum("td,te->de", normed, grad_tok_k, preferred_element_type=jnp.float32),
            jnp.einsum("td,te->de", normed, grad_tok_v, preferred_element_type=jnp.float32),
        ],
        axis=1,
    )
    grad_normed = jnp.einsum(
        "te,de->td", grad_tok_q, qkv_weight[:, :features], preferred_element_type=jnp.float32
    )
    grad_normed = grad_normed + jnp.einsum(
        "te,de->td",
        grad_tok_k,
        qkv_weight[:, features : 2 * features],
        preferred_element_type=jnp.float32,
    )
    grad_normed = grad_normed + jnp.einsum(
        "te,de->td", grad_tok_v, qkv_weight[:, 2 * features :], preferred_element_type=jnp.float32
    )
    _, first_pull = jax.vjp(norm_rows, flat_in, attn_gain)
    grad_input, grad_attn_gain = first_pull(grad_normed)
    grad_input = (
        (grad_input + grad_hidden).astype(jnp.bfloat16).reshape(doc_count, row_count, features)
    )
    summed = lax.psum(
        (grad_attn_gain, grad_qkv, grad_attn_out, grad_mlp_gain, grad_mlp_in, grad_mlp_out),
        ("doc", "seq"),
    )
    return (output, grad_input, summed[0], summed[1], summed[2], summed[3], summed[4], summed[5])


def solution(mesh):
    placed = (P("doc", "seq", None), P(), P(), P(), P(), P(), P(), P("doc", "seq", None))
    return jax.shard_map(
        per_device,
        mesh=mesh,
        in_specs=placed,
        out_specs=(P("doc", "seq", None), P("doc", "seq", None), P(), P(), P(), P(), P(), P()),
        check_vma=False,
    )
```

profile of v0, /device:TPU:0, one launch (start us, length us, event | category | flops | bytes accessed | tf_op | source)
XLA Modules:
  0.0 743.6 jit_solution(14533819958164597936)
XLA Ops:
  12.8 4.3 fusion.13
  23.3 6.3 all-to-all-start
  29.6 3.9 fusion.58
  59.2 5.0 add_convert_fusion.3
  67.2 5.1 all-to-all-start.1
  75.3 16.6 %all-to-all-done.1 = bf16[2,256,768]{1,0,2:T(2,128)(2,1)} async-done(((bf16[2,256,768]{1,0,2:T(2,128)(2,1)}), bf16[2,256,768]{1,0,2:T(2,128)(2,1)}, u32[]{:S(2)}, u32[]{:S(2)}) %all-to-all-start.1) | async-done | bytes 786464 | tf_op jit(solution)/shard_map/all_to_all | solution.py:150
  91.9 4.7 all-to-all-start.2
  101.1 15.2 %all-to-all-done.2 = bf16[2,256,768]{1,0,2:T(2,128)(2,1)} async-done(((bf16[2,256,768]{1,0,2:T(2,128)(2,1)}), bf16[2,256,768]{1,0,2:T(2,128)(2,1)}, u32[]{:S(2)}, u32[]{:S(2)}) %all-to-all-start.2) | async-done | bytes 786464 | tf_op jit(solution)/shard_map/all_to_all | solution.py:151
  119.5 19.5 %while.26 = (s32[]{:T(128)}, bf16[2,1024,192]{1,2,0:T(8,128)(2,1)}, f32[2,3,1024]{2,1,0:T(4,128)}, bf16[2,1024,192]{1,2,0:T(8,128)(2,1)}, bf16[2,1024,192]{1,2,0...) while((s32[]{:T(128)}, bf16[2,1024,192]{1,2,0:T(8,128)(2,1)}, f32[2,3,1024]{2,1,0:T(4,128)}, ...), condition=%wide.region_5.6_spmd, body=%wide.region_2.5_spmd.sunk | while | flops 833811456 | bytes 48861340 | solution.py:154
  142.7 29.5 %all_to_all.132 = bf16[2,1024,192]{2,0,1:T(2,128)(2,1)} all-to-all(bf16[2,1024,192]{2,0,1:T(2,128)(2,1)} %copy.86), channel_id=1, replica_groups=mesh['doc'=8,'seq'=4] {'seq'}, dimensions={1} | all-to-all | bytes 1572864 | tf_op jit(solution)/shard_map/all_to_all | solution.py:157
  172.2 5.8 copy.87
  184.6 5.6 fusion.39
  205.9 17.4 %all-to-all-done.4 = bf16[2,256,768]{1,0,2:T(2,128)(2,1)S(1)} async-done(((bf16[2,256,768]{1,0,2:T(2,128)(2,1)}), bf16[2,256,768]{1,0,2:T(2,128)(2,1)S(1)}, u32[]{:S(2)}, u32[]{:S(2)}) %all-to-all-start.4) | async-done | bytes 786464 | tf_op jit(solution)/shard_map/all_to_all | solution.py:190
  227.3 60.3 %while.27 = (s32[]{:T(128)}, bf16[2,1024,192]{1,2,0:T(8,128)(2,1)}, bf16[2,1024,192]{1,2,0:T(8,128)(2,1)}, bf16[2,1024,192]{1,2,0:T(8,128)(2,1)}, bf16[2,1024,19...) while((s32[]{:T(128)}, bf16[2,1024,192]{1,2,0:T(8,128)(2,1)}, ...), condition=%wide.region_12.13_spmd, body=%wide.region_10.12_spmd.sunk | while | flops 2053501952 | bytes 154489168 | solution.py:192
  238.7 3.7 multiply_reduce_fusion.8
  242.5 5.3 multiply_convert_fusion.6
  247.7 4.1 convolution_bitcast_fusion.3
  268.9 3.7 multiply_reduce_fusion.8
  272.6 5.3 multiply_convert_fusion.6
  277.9 4.1 convolution_bitcast_fusion.3
  296.9 23.1 %all-to-all-done.7 = bf16[2,1024,192]{2,0,1:T(2,128)(2,1)S(1)} async-done(((bf16[2,1024,192]{2,0,1:T(2,128)(2,1)}), bf16[2,1024,192]{2,0,1:T(2,128)(2,1)S(1)}, u32[]{:S(2)}, u32[]{:S(2)}) %all-to-all-start.7) | async-done | bytes 786464 | tf_op jit(solution)/shard_map/all_to_all | solution.py:199
  325.6 23.1 %all-to-all-done.5 = bf16[2,1024,192]{2,0,1:T(2,128)(2,1)S(1)} async-done(((bf16[2,1024,192]{2,0,1:T(2,128)(2,1)}), bf16[2,1024,192]{2,0,1:T(2,128)(2,1)S(1)}, u32[]{:S(2)}, u32[]{:S(2)}) %all-to-all-start.5) | async-done | bytes 786464 | tf_op jit(solution)/shard_map/all_to_all | solution.py:197
  348.7 4.2 all-to-all-start.6
  361.3 5.2 fusion.40
  366.4 4.7 copy.96
  372.2 5.7 copy.92
  380.2 5.7 copy.94
  395.2 4.0 add_convert_fusion.2
  404.1 43.1 %all-reduce.2 = (f32[768]{0:T(1024)}, f32[768]{0:T(1024)}) all-reduce(f32[768]{0:T(1024)S(1)} %get-tuple-element.139, f32[768]{0:T(1024)S(1)} %copy-done.49), channel_id=1, replica_groups=mesh['doc'=8,'seq'=4] {'doc','seq'}, use_global_device_ids=true, to_apply=%region_16.17 | all-reduce | flops 1536 | bytes 12288 | tf_op jit(solution)/shard_map/psum | solution.py:229
  450.1 268.5 %all-reduce.6.cloned.1.call-done = (f32[768,2304]{0,1:T(8,128)}, f32[768,768]{1,0:T(8,128)}, f32[768,2304]{1,0:T(8,128)}, f32[1152,768]{1,0:T(8,128)}) async-done(((f32[768,2304]{0,1:T(8,128)}, f32[768,768]{1,0:T(8,128)}, f32[768,2304]{1,0:T(8,128)}, f32[1152,768]{1,0:T(8,128)}), (f32[768,2304]{0,1:T(8,128)}, f32[768,768]{1,0:T(8,128)}, f32[768,2304]{1,0:T(8,128)}, ...) | async-done | bytes 20054032 | tf_op jit(solution)/shard_map/psum | solution.py:229
  718.6 8.1 %copy.97 = f32[768,2304]{1,0:T(8,128)} copy(f32[768,2304]{0,1:T(8,128)} %get-tuple-element.177) | data formatting | bytes 14155776
  728.1 6.6 copy.145
  (252 shorter events, 180.6 us)
Async XLA Ops:
  7.2 175.2 %copy-start = (bf16[768,2304]{1,0:T(8,128)(2,1)S(1)}, bf16[768,2304]{1,0:T(8,128)(2,1)}, u32[]{:S(2)}) copy-start(bf16[768,2304]{1,0:T(8,128)(2,1)} %param.17) | copy-start | bytes 10616836
  12.8 4.3 copy-start.8
  23.3 43.9 %all-to-all-start = ((bf16[2,256,768]{1,0,2:T(2,128)(2,1)}), bf16[2,256,768]{1,0,2:T(2,128)(2,1)}, u32[]{:S(2)}, u32[]{:S(2)}) async-start(bf16[2,256,768]{1,0,2:T(2,128)(2,1)} %copy.71), calls=%async_computation | async-start | bytes 1572864 | tf_op jit(solution)/shard_map/all_to_all | solution.py:152
  33.5 8.8 %copy-start.50 = (f32[32]{0:T(128)}, f32[32]{0:T(128)S(1)}, u32[]{:S(2)}) copy-start(f32[32]{0:T(128)S(1)} %multiply_power_fusion) | copy-start | bytes 388
  67.2 24.7 %all-to-all-start.1 = ((bf16[2,256,768]{1,0,2:T(2,128)(2,1)}), bf16[2,256,768]{1,0,2:T(2,128)(2,1)}, u32[]{:S(2)}, u32[]{:S(2)}) async-start(bf16[2,256,768]{1,0,2:T(2,128)(2,1)} %copy.78), calls=%async_computation.1 | async-start | bytes 1572864 | tf_op jit(solution)/shard_map/all_to_all | solution.py:150
  91.9 24.4 %all-to-all-start.2 = ((bf16[2,256,768]{1,0,2:T(2,128)(2,1)}), bf16[2,256,768]{1,0,2:T(2,128)(2,1)}, u32[]{:S(2)}, u32[]{:S(2)}) async-start(bf16[2,256,768]{1,0,2:T(2,128)(2,1)} %copy.83), calls=%async_computation.2 | async-start | bytes 1572864 | tf_op jit(solution)/shard_map/all_to_all | solution.py:151
  182.1 13.2 %copy-start.6 = (f32[512,768]{1,0:T(8,128)}, f32[512,768]{1,0:T(8,128)S(1)}, u32[]{:S(2)}) copy-start(f32[512,768]{1,0:T(8,128)S(1)} %get-tuple-element.225) | copy-start | bytes 4718596
  182.1 13.2 %copy-start.41 = (f32[512]{0:T(512)}, f32[512]{0:T(512)S(1)}, u32[]{:S(2)}) copy-start(f32[512]{0:T(512)S(1)} %broadcast_multiply_fusion.3) | copy-start | bytes 6148
  182.4 12.8 %copy-start.43 = (f32[512]{0:T(512)}, f32[512]{0:T(512)S(1)}, u32[]{:S(2)}) copy-start(f32[512]{0:T(512)S(1)} %fusion.46) | copy-start | bytes 6148
  198.8 5.3 copy-start.51
  200.6 22.6 %all-to-all-start.4 = ((bf16[2,256,768]{1,0,2:T(2,128)(2,1)}), bf16[2,256,768]{1,0,2:T(2,128)(2,1)S(1)}, u32[]{:S(2)}, u32[]{:S(2)}) async-start(bf16[2,256,768]{1,0,2:T(2,128)(2,1)} %copy.88), calls=%async_computation.4 | async-start | bytes 1572864 | tf_op jit(solution)/shard_map/all_to_all | solution.py:190
  247.7 4.6 copy-start.2
  277.9 4.6 copy-start.2
  287.6 7.2 copy-start.22
  291.3 28.7 %all-to-all-start.7 = ((bf16[2,1024,192]{2,0,1:T(2,128)(2,1)}), bf16[2,1024,192]{2,0,1:T(2,128)(2,1)S(1)}, u32[]{:S(2)}, u32[]{:S(2)}) async-start(bf16[2,1024,192]{2,0,1:T(2,128)(2,1)} %copy.95), calls=%async_computation.7 | async-start | bytes 2097152 | tf_op jit(solution)/shard_map/all_to_all | solution.py:199
  294.9 28.7 %copy-start.25 = (bf16[2,1024,192]{1,2,0:T(8,128)(2,1)S(1)}, bf16[2,1024,192]{1,2,0:T(8,128)(2,1)}, u32[]{:S(2)}) copy-start(bf16[2,1024,192]{1,2,0:T(8,128)(2,1)} %get-tuple-element.103) | copy-start | bytes 2359300
  320.0 28.7 %copy-start.17 = (bf16[2,1024,192]{2,0,1:T(2,128)(2,1)}, bf16[2,1024,192]{2,0,1:T(2,128)(2,1)S(1)}, u32[]{:S(2)}) copy-start(bf16[2,1024,192]{2,0,1:T(2,128)(2,1)S(1)} %all-to-all-done.7) | copy-start | bytes 2359300
  320.0 28.7 %all-to-all-start.5 = ((bf16[2,1024,192]{2,0,1:T(2,128)(2,1)}), bf16[2,1024,192]{2,0,1:T(2,128)(2,1)S(1)}, u32[]{:S(2)}, u32[]{:S(2)}) async-start(bf16[2,1024,192]{2,0,1:T(2,128)(2,1)} %copy.91), calls=%async_computation.5 | async-start | bytes 2097152 | tf_op jit(solution)/shard_map/all_to_all | solution.py:197
  348.7 8.4 %copy-start.18 = (bf16[2,1024,192]{2,0,1:T(2,128)(2,1)}, bf16[2,1024,192]{2,0,1:T(2,128)(2,1)S(1)}, u32[]{:S(2)}) copy-start(bf16[2,1024,192]{2,0,1:T(2,128)(2,1)S(1)} %all-to-all-done.5) | copy-start | bytes 2359300
  348.7 31.4 %all-to-all-start.6 = ((bf16[2,1024,192]{2,0,1:T(2,128)(2,1)}), bf16[2,1024,192]{2,0,1:T(2,128)(2,1)}, u32[]{:S(2)}, u32[]{:S(2)}) async-start(bf16[2,1024,192]{2,0,1:T(2,128)(2,1)} %copy.93), calls=%async_computation.6 | async-start | bytes 2097152 | tf_op jit(solution)/shard_map/all_to_all | solution.py:198
  353.0 4.1 copy-start.14
  353.0 365.6 %all-reduce.6.cloned.1.call-start = ((), (), s32[]{:S(2)}) async-start(), calls=%async_computation.8 | async-start | bytes 40108032 | tf_op jit(solution)/shard_map/psum | solution.py:229
  357.1 4.1 copy-start.36
  357.2 4.1 copy-start.39
  357.2 4.1 copy-start.42
  357.2 4.1 copy-start.44
  377.9 9.3 %copy-start.9 = (bf16[2,256,768]{2,1,0:T(8,128)(2,1)S(1)}, bf16[2,256,768]{2,1,0:T(8,128)(2,1)}, u32[]{:S(2)}) copy-start(bf16[2,256,768]{2,1,0:T(8,128)(2,1)} %copy-done.8) | copy-start | bytes 2359300
  395.2 4.1 copy-start.30
  403.3 43.9 %copy-start.46 = (f32[512]{0:T(512)S(1)}, f32[512]{0:T(512)}, u32[]{:S(2)}) copy-start(f32[512]{0:T(512)} %copy-done.45) | copy-start | bytes 6148
  718.6 8.1 %copy-start.34 = (f32[768,768]{1,0:T(8,128)S(1)}, f32[768,768]{1,0:T(8,128)}, u32[]{:S(2)}) copy-start(f32[768,768]{1,0:T(8,128)} %get-tuple-element.433) | copy-start | bytes 7077892
  728.1 6.6 copy-start.19
  728.1 8.4 %copy-start.1 = (bf16[768,2304]{1,0:T(8,128)(2,1)S(1)}, bf16[768,2304]{1,0:T(8,128)(2,1)}, u32[]{:S(2)}) copy-start(bf16[768,2304]{1,0:T(8,128)(2,1)} %param.17) | copy-start | bytes 10616836
  (38 other events, 68.4 us)
Sparse Core Ops, SparseCore 0:
  394.7 323.8 all-reduce.5
where the time goes:
time: 752 us; the launch traced here: 744 us
  waiting for transfers between devices  364 us (48%)
  local copies, waits for them, and re-layouts  133 us (18%)
  matrix products  77.7 us (10%)
  blocking collectives  72.6 us (10%)
  other arithmetic  49.6 us (7%)
  starting transfers between devices  31.3 us (4%)
  between operations  14.9 us (2%)
    psum x1, waiting for transfers between devices, per_device(): lax.psum((grad_attn_gain, grad_qkv, grad_attn_out, grad_mlp_gain, grad_ml...  268 us
    psum x1, blocking collectives, per_device(): lax.psum((grad_attn_gain, grad_qkv, grad_attn_out, grad_mlp_gain, grad_ml...  43.1 us
    unnamed x102, local copies, waits for them, and re-layouts  30.9 us
    all_to_all x1, blocking collectives, per_device(): lax.all_to_all(mixed_heads, 'seq', split_axis=1, concat_axis=2, tiled=True)  29.5 us
    all_to_all x1, waiting for transfers between devices, per_device(): lax.all_to_all(grad_head_v, 'seq', split_axis=1, concat_axis=2, tiled=True)  23.1 us
    all_to_all x1, waiting for transfers between devices, per_device(): lax.all_to_all(grad_head_q, 'seq', split_axis=1, concat_axis=2, tiled=True)  23.1 us
    all_to_all x1, waiting for transfers between devices, per_device(): lax.all_to_all(grad_attended, 'seq', split_axis=2, concat_axis=1, tiled=T...  17.4 us
    all_to_all x1, waiting for transfers between devices, per_device(): lax.all_to_all(queries, 'seq', split_axis=2, concat_axis=1, tiled=True)  16.6 us
  transfers between devices with their start and end apart: 8, of which 6 were waited for; matrix products, arithmetic and copies ran while one was open for 12% of the time, Pallas kernels for 0%

commit v1 on v0

v1 whole, which is shorter than its diff:
```python
import functools

import jax
import jax.numpy as jnp
import numpy as np
from jax import lax
from jax.experimental import pallas as pl
from jax.experimental.pallas import tpu as pltpu
from jax.sharding import PartitionSpec as P

HEAD_DIM = 64
ROPE_THETA = 160000.0
NORM_EPSILON = 1e-05
F32 = jnp.float32
BF16 = jnp.bfloat16
MESH = pl.DeviceIdType.MESH
LANES = 128
VMEM_LIMIT = 60 << 20


def nn(a, b):
    return lax.dot_general(a, b, (((1,), (0,)), ((), ())), preferred_element_type=F32)


def nt(a, b):
    return lax.dot_general(a, b, (((1,), (1,)), ((), ())), preferred_element_type=F32)


def lane_of(shape):
    return lax.broadcasted_iota(jnp.int32, shape, 1)


def one_head(pair, sub):
    lane = lane_of(pair.shape)
    mine = (lane < HEAD_DIM) if sub == 0 else (lane >= HEAD_DIM)
    return jnp.where(mine, pair, jnp.zeros_like(pair))


def turned(values):
    back = pltpu.roll(values, HEAD_DIM // 2, 1)
    ahead = pltpu.roll(values, LANES - HEAD_DIM // 2, 1)
    return jnp.where(lane_of(values.shape) % HEAD_DIM < HEAD_DIM // 2, ahead, back)


def row_stats(values):
    mean = jnp.mean(values, axis=1, keepdims=True)
    centered = values - mean
    scale = lax.rsqrt(jnp.mean(centered * centered, axis=1, keepdims=True) + NORM_EPSILON)
    return centered * scale, scale


def norm_back(grad, unit, scale, gain):
    weighted = grad * gain
    along = jnp.mean(weighted, axis=1, keepdims=True)
    across = jnp.mean(weighted * unit, axis=1, keepdims=True)
    return scale * (weighted - along - unit * across)


def bit_of(index, weight):
    return (index // weight) % 2


def flipped(index, weight):
    return index + weight - 2 * weight * bit_of(index, weight)


def greet(partners):
    barrier = pltpu.get_barrier_semaphore()
    for partner in partners:
        pl.semaphore_signal(barrier, inc=1, device_id=partner, device_id_type=MESH)
    pl.semaphore_wait(barrier, len(partners))


def group_partners(doc, seq, n_seq):
    core = doc % 2
    found = []
    for other_core in range(2):
        for step in range(n_seq):
            if other_core == 0 and step == 0:
                continue
            found.append(
                (doc - core + (core + other_core) % 2, (seq + step) % n_seq)
            )
    return found


class Exchange:
    def __init__(self, doc, seq, n_seq):
        core = doc % 2
        half = n_seq // 2
        base = doc - core
        self.out_targets = [(base + seq // half, 2 * core + block) for block in range(2)]
        self.out_slot = seq % half
        self.back_targets = [(base + seq // 2, half * core + slot) for slot in range(2)]
        self.back_block = seq % 2
        self.doc, self.seq = doc, seq

    def is_self(self, target):
        return jnp.logical_and(target[0] == self.doc, target[1] == self.seq)


def send_or_keep(ex, target, src, dst, send_sem, recv_sem):
    mine = ex.is_self(target)

    @pl.when(mine)
    def _():
        pltpu.make_async_copy(src, dst, recv_sem).start()

    @pl.when(jnp.logical_not(mine))
    def _():
        pltpu.make_async_remote_copy(
            src_ref=src, dst_ref=dst, send_sem=send_sem, recv_sem=recv_sem,
            device_id=target, device_id_type=MESH,
        ).start()


def wait_sent(ex, target, src, dst, send_sem, recv_sem):
    @pl.when(jnp.logical_not(ex.is_self(target)))
    def _():
        pltpu.make_async_remote_copy(
            src_ref=src, dst_ref=dst, send_sem=send_sem, recv_sem=recv_sem,
            device_id=target, device_id_type=MESH,
        ).wait_send()


def wait_bytes(ref, sem):
    pltpu.make_async_copy(ref, ref, sem).wait()


def front_kernel(
    n_seq,
    x_in, cot_in, gain1, gain2, wqkv_in, wo_in, win_in, wout_in, cos_in, sin_in,
    out_o, x_o, xn_o, q_o, k_o, v_o, do_o, lse_o, dd_o, dh_o, g_o,
    xs, cs, outs, wqkv, wo, win, wout, cos, sin, xn, q, k, v, att, h, xn2, xn2t, hid, dgu, dmt, grads, do, dh, lse, dd, acc,
    w_sem, send_sem, recv_sem, kv_send, kv_recv, out_sem,
):
    doc, seq = lax.axis_index("doc"), lax.axis_index("seq")
    core = doc % 2
    ex = Exchange(doc, seq, n_seq)
    rows = x_in.shape[1]
    tokens, width = xs.shape
    ff = wout.shape[0]
    pairs = width // LANES

    loads = [
        pltpu.make_async_copy(s, d, w_sem.at[i])
        for i, (s, d) in enumerate(
            [(wqkv_in, wqkv), (wo_in, wo), (win_in, win), (wout_in, wout)]
            + [(t.at[pl.ds(core * tokens, tokens)], d) for t, d in ((cos_in, cos), (sin_in, sin))]
        )
    ]
    for load in loads:
        load.start()
    greet(group_partners(doc, seq, n_seq))

    def spread(src, dst, base):
        for block in range(2):
            send_or_keep(
                ex, ex.out_targets[block], src.at[block],
                dst.at[pl.ds(ex.out_slot * rows, rows)],
                send_sem.at[base + block], recv_sem.at[base + ex.out_slot],
            )

    def spread_sent(src, dst, base):
        for block in range(2):
            wait_sent(
                ex, ex.out_targets[block], src.at[block],
                dst.at[pl.ds(ex.out_slot * rows, rows)],
                send_sem.at[base + block], recv_sem.at[base + ex.out_slot],
            )

    spread(x_in, xs, 0)
    for slot in range(2):
        wait_bytes(xs.at[pl.ds(slot * rows, rows)], recv_sem.at[slot])
    spread(cot_in, cs, 2)

    unit, _ = row_stats(xs[...].astype(F32))
    xn[...] = (unit * gain1[...]).astype(BF16)
    for i in (0, 4, 5):
        loads[i].wait()

    def roped(tile, scale):
        return ((tile * cos[...] + turned(tile) * sin[...]) * scale).astype(BF16)

    def project(j, _):
        lanes = pl.ds(pl.multiple_of(j * LANES, LANES), LANES)
        k_lanes = pl.ds(pl.multiple_of(width + j * LANES, LANES), LANES)
        v_lanes = pl.ds(pl.multiple_of(2 * width + j * LANES, LANES), LANES)
        k[:tokens, lanes] = roped(nn(xn[...], wqkv[:, k_lanes]), 1.0)
        v[:tokens, lanes] = nn(xn[...], wqkv[:, v_lanes]).astype(BF16)
        return 0

    lax.fori_loop(0, pairs, project, 0)
    sibling = (flipped(doc, 1), seq)
    kv_copies = [
        pltpu.make_async_remote_copy(
            src_ref=ref.at[pl.ds(0, tokens)], dst_ref=ref.at[pl.ds(tokens, tokens)],
            send_sem=kv_send.at[i], recv_sem=kv_recv.at[i],
            device_id=sibling, device_id_type=MESH,
        )
        for i, ref in enumerate((k, v))
    ]
    for copy in kv_copies:
        copy.start()

    def project_q(j, _):
        lanes = pl.ds(pl.multiple_of(j * LANES, LANES), LANES)
        q[:, lanes] = roped(nn(xn[...], wqkv[:, lanes]), 0.125)
        return 0

    lax.fori_loop(0, pairs, project_q, 0)
    for copy in kv_copies:
        copy.wait()

    def attend(j, _):
        lanes = pl.ds(pl.multiple_of(j * LANES, LANES), LANES)
        k2, vt, q2 = k[:, lanes], v[:, lanes].T, q[:, lanes]
        mixed = []
        for sub in range(2):
            scores = nt(one_head(k2, sub), q2)
            top = jnp.max(scores, axis=0, keepdims=True)
            weights = jnp.exp(scores - top)
            total = jnp.sum(weights, axis=0, keepdims=True)
            lse[j, sub : sub + 1, :] = top + jnp.log(total)
            mixed.append(
                nn(vt[sub * HEAD_DIM : (sub + 1) * HEAD_DIM], weights.astype(BF16)) * (1.0 / total)
            )
        att[:, lanes] = jnp.concatenate(mixed, axis=0).T.astype(BF16)
        return 0

    lax.fori_loop(0, pairs, attend, 0)

    loads[1].wait()
    h[...] = xs[...].astype(F32) + nn(att[...], wo[...])
    unit2, _ = row_stats(h[...])
    xn2[...] = (unit2 * gain2[...]).astype(BF16)
    xn2t[...] = xn2[...].T
    loads[2].wait()
    loads[3].wait()
    for slot in range(2):
        wait_bytes(cs.at[pl.ds(slot * rows, rows)], recv_sem.at[2 + slot])
    dmt[...] = cs[...].T

    def feed(j, _):
        gate_lanes = pl.ds(pl.multiple_of(j * LANES, LANES), LANES)
        up_lanes = pl.ds(pl.multiple_of(ff + j * LANES, LANES), LANES)
        gate = nn(xn2[...], win[:, gate_lanes])
        up = nn(xn2[...], win[:, up_lanes])
        phi = 0.5 * (1.0 + lax.erf(gate * 0.7071067811865476))
        slope = phi + gate * (0.3989422804014327 * jnp.exp(-0.5 * gate * gate))
        active = gate * phi
        hid[:, gate_lanes] = (active * up).astype(BF16)
        dhid = nt(cs[...], wout[pl.ds(pl.multiple_of(j * LANES, LANES), LANES), :])
        dgu[:, gate_lanes] = (dhid * up * slope).astype(BF16)
        dgu[:, up_lanes] = (dhid * active).astype(BF16)
        return 0

    lax.fori_loop(0, ff // LANES, feed, 0)

    outs[...] = (h[...] + nn(hid[...], wout[...])).astype(BF16)
    for slot in range(2):
        send_or_keep(
            ex, ex.back_targets[slot], outs.at[pl.ds(slot * rows, rows)],
            out_o.at[ex.back_block], send_sem.at[4 + slot], recv_sem.at[4 + ex.back_block],
        )

    step = 3 * LANES

    def grad_out(j, _):
        lanes = pl.ds(pl.multiple_of(j * step, LANES), step)
        grads[:, lanes] = nn(dmt[...], hid[:, lanes]).astype(BF16)
        return 0

    lax.fori_loop(0, ff // step, grad_out, 0)

    def grad_in(j, _):
        lanes = pl.ds(pl.multiple_of(j * step, LANES), step)
        g_lanes = pl.ds(pl.multiple_of(ff + j * step, LANES), step)
        grads[:, g_lanes] = nn(xn2t[...], dgu[:, lanes]).astype(BF16)
        return 0

    lax.fori_loop(0, 2 * ff // step, grad_in, 0)

    acc[...] = nt(dgu[...], win[...])
    unit2, scale2 = row_stats(h[...])
    grad2 = acc[...]
    dh[...] = cs[...].astype(F32) + norm_back(grad2, unit2, scale2, gain2[...])
    gain_terms = (grad2 * unit2).astype(BF16).T
    grads[:, 3 * ff + width :] = nn(gain_terms, jnp.ones((tokens, LANES), BF16)).astype(BF16)
    datt = dh[...].astype(BF16)
    att_t = att[...].T
    grads[:, 3 * ff : 3 * ff + width] = nn(att_t, datt).astype(BF16)
    do[...] = nt(datt, wo[...]).astype(BF16)

    lane = lax.broadcasted_iota(jnp.int32, (8, LANES), 1)
    row = lax.broadcasted_iota(jnp.int32, (8, LANES), 0)
    pick = jnp.where(lane // HEAD_DIM == row, 1.0, 0.0).astype(F32)
    for j in range(pairs):
        lanes = slice(j * LANES, (j + 1) * LANES)
        product = do[:, lanes].astype(F32) * att[:, lanes].astype(F32)
        sums = lax.dot_general(
            pick, product, (((1,), (1,)), ((), ())),
            precision=lax.Precision.HIGHEST, preferred_element_type=F32,
        )
        dd[j] = sums[:2]

    stores = [
        pltpu.make_async_copy(s, d, out_sem.at[i])
        for i, (s, d) in enumerate(
            [(xs, x_o), (xn, xn_o), (q, q_o), (k, k_o), (v, v_o), (do, do_o), (lse, lse_o), (dd, dd_o), (dh, dh_o), (grads, g_o)]
        )
    ]
    for store in stores:
        store.start()
    spread_sent(x_in, xs, 0)
    spread_sent(cot_in, cs, 2)
    for block in range(2):
        wait_bytes(out_o.at[block], recv_sem.at[4 + block])
    for slot in range(2):
        wait_sent(
            ex, ex.back_targets[slot], outs.at[pl.ds(slot * rows, rows)],
            out_o.at[ex.back_block], send_sem.at[4 + slot], recv_sem.at[4 + ex.back_block],
        )
    for store in stores:
        store.wait()


def front(n_seq, inputs, cotangent, gain1, gain2, wqkv, wo, win, wout, cos, sin):
    blocks, rows, width = inputs.shape
    tokens = blocks * rows
    ff = wout.shape[0]
    pairs = width // LANES
    cols = 3 * ff + width + LANES
    hbm, vmem = pl.BlockSpec(memory_space=pl.ANY), pl.BlockSpec(memory_space=pltpu.VMEM)
    sds = jax.ShapeDtypeStruct
    return pl.pallas_call(
        functools.partial(front_kernel, n_seq),
        out_shape=[
            sds((blocks, rows, width), BF16), sds((tokens, width), BF16), sds((tokens, width), BF16),
            sds((tokens, width), BF16), sds((2 * tokens, width), BF16), sds((2 * tokens, width), BF16),
            sds((tokens, width), BF16), sds((pairs, 2, tokens), F32), sds((pairs, 2, tokens), F32),
            sds((tokens, width), F32), sds((width, cols), BF16),
        ],
        in_specs=[hbm, hbm, vmem, vmem] + [hbm] * 6,
        out_specs=[hbm] * 11,
        scratch_shapes=[
            pltpu.VMEM((tokens, width), BF16), pltpu.VMEM((tokens, width), BF16), pltpu.VMEM((tokens, width), BF16),
            pltpu.VMEM(wqkv.shape, BF16), pltpu.VMEM(wo.shape, BF16), pltpu.VMEM(win.shape, BF16), pltpu.VMEM(wout.shape, BF16),
            pltpu.VMEM((tokens, LANES), F32), pltpu.VMEM((tokens, LANES), F32),
            pltpu.VMEM((tokens, width), BF16), pltpu.VMEM((tokens, width), BF16),
            pltpu.VMEM((2 * tokens, width), BF16), pltpu.VMEM((2 * tokens, width), BF16),
            pltpu.VMEM((tokens, width), BF16), pltpu.VMEM((tokens, width), F32),
            pltpu.VMEM((tokens, width), BF16), pltpu.VMEM((width, tokens), BF16),
            pltpu.VMEM((tokens, ff), BF16), pltpu.VMEM((tokens, 2 * ff), BF16), pltpu.VMEM((width, tokens), BF16),
            pltpu.VMEM((width, cols), BF16), pltpu.VMEM((tokens, width), BF16), pltpu.VMEM((tokens, width), F32),
            pltpu.VMEM((pairs, 2, tokens), F32), pltpu.VMEM((pairs, 2, tokens), F32),
            pltpu.VMEM((tokens, width), F32),
            pltpu.SemaphoreType.DMA((6,)), pltpu.SemaphoreType.DMA((6,)), pltpu.SemaphoreType.DMA((6,)),
            pltpu.SemaphoreType.DMA((2,)), pltpu.SemaphoreType.DMA((2,)), pltpu.SemaphoreType.DMA((10,)),
        ],
        compiler_params=pltpu.CompilerParams(collective_id=0, has_side_effects=True, vmem_limit_bytes=VMEM_LIMIT),
        name="front",
    )(inputs, cotangent, gain1, gain2, wqkv, wo, win, wout, cos, sin)


class Reduction:
    def __init__(self, rows, src, lanes, width, acc, landing, final, sems, partners, weights, out):
        self.src, self.lanes, self.width = src, lanes, width
        self.acc, self.landing, self.final, self.sems, self.out = acc, landing, final, sems, out
        self.core, self.bits, self.partners = weights[0], weights[1:], partners
        self.rows = rows
        self.plan = []
        offset, extent, base = 0, rows, rows
        for bit in self.bits:
            split = (extent // 2) % 16 == 0
            keep = extent // 2 if split else extent
            self.plan.append((offset, extent, keep, split, base))
            base += keep
            if split:
                offset = offset + bit * keep
            extent = keep
        self.final_offset, self.final_extent = offset, extent
        self.rounds = len(self.bits)

    @staticmethod
    def landing_rows(rows, rounds):
        total, extent = rows, rows
        for _ in range(rounds):
            extent = extent // 2 if (extent // 2) % 16 == 0 else extent
            total += extent
        return total

    def part(self, which):
        return pl.ds(pl.multiple_of(self.lanes[0] + which * self.lanes[1], LANES), self.width)

    def rows_at(self, start, extent):
        return pl.ds(pl.multiple_of(start, 16) if not isinstance(start, int) else start, extent)

    def copy(self, src, dst, slot, partner):
        return pltpu.make_async_remote_copy(
            src_ref=src, dst_ref=dst, send_sem=self.sems[0].at[slot], recv_sem=self.sems[1].at[slot],
            device_id=partner, device_id_type=MESH,
        )

    def core_copy(self):
        return self.copy(
            self.src.at[:, self.part(1 - self.core)], self.landing.at[pl.ds(0, self.rows)], 0, self.partners[0]
        )

    def own_copy(self):
        return pltpu.make_async_copy(self.src.at[:, self.part(self.core)], self.acc, self.sems[2])

    def down_copy(self, r):
        offset, extent, keep, split, base = self.plan[r]
        start = offset + (1 - self.bits[r]) * keep if split else offset
        return self.copy(
            self.acc.at[self.rows_at(start, keep)], self.landing.at[pl.ds(base, keep)], 1 + r, self.partners[1 + r]
        )

    def up_copy(self, r):
        offset, extent, keep, split, base = self.plan[r]
        start = self.rows_at(offset + self.bits[r] * keep, keep)
        return self.copy(self.final.at[start], self.final.at[start], 1 + self.rounds + r, self.partners[1 + r])

    def up_wait(self, r):
        offset, extent, keep, split, base = self.plan[r]
        start = self.rows_at(offset + (1 - self.bits[r]) * keep, keep)
        copy = self.copy(self.final.at[start], self.final.at[start], 1 + self.rounds + r, self.partners[1 + r])
        copy.wait_recv()
        self.up_copy(r).wait_send()

    def last_copy(self):
        return self.copy(self.final, self.out.at[:, self.part(self.core)], 1 + 2 * self.rounds, self.partners[0])

    def last_own(self):
        return pltpu.make_async_copy(self.final, self.out.at[:, self.part(self.core)], self.sems[2])

    def add(self, offset, base, keep, target):
        block = 96
        while keep % block:
            block //= 2

        def body(i, _):
            mine = self.rows_at(offset + i * block, block)
            theirs = pl.ds(pl.multiple_of(base + i * block, 16), block)
            target[mine] = (self.acc[mine].astype(F32) + self.landing[theirs].astype(F32)).astype(BF16)
            return 0

        lax.fori_loop(0, keep // block, body, 0)

    def start(self):
        self.core_copy().start()
        self.own_copy().start()

    def steps(self):
        ups = [r for r in reversed(range(self.rounds)) if self.plan[r][3]]

        def core_done():
            self.core_copy().wait()
            self.own_copy().wait()
            self.add(0, 0, self.rows, self.acc)
            self.down_copy(0).start()

        def down_done(r):
            offset, extent, keep, split, base = self.plan[r]
            self.down_copy(r).wait()
            target = self.acc if r + 1 < self.rounds else self.final
            self.add(offset + self.bits[r] * keep if split else offset, base, keep, target)
            if r + 1 < self.rounds:
                self.down_copy(r + 1).start()
            else:
                self.up_copy(ups[0]).start()

        def up_done(i):
            self.up_wait(ups[i])
            if i + 1 < len(ups):
                self.up_copy(ups[i + 1]).start()
            else:
                self.last_copy().start()
                self.last_own().start()

        def last_done():
            copy = self.copy(
                self.final, self.out.at[:, self.part(1 - self.core)], 1 + 2 * self.rounds, self.partners[0]
            )
            copy.wait_recv()
            self.last_copy().wait_send()
            self.last_own().wait()

        return (
            [core_done]
            + [functools.partial(down_done, r) for r in range(self.rounds)]
            + [functools.partial(up_done, i) for i in range(len(ups))]
            + [last_done]
        )


def log2(n):
    return n.bit_length() - 1


def back_kernel(
    n_doc, n_seq,
    x_in, xn_in, q_in, k_in, v_in, do_in, lse_in, dd_in, dh_in, g1_in, wqkv_in, gain1, cos_in, sin_in,
    dx_o, g1_o, g2_o,
    xs, xn, q, k, v, do, lse, dd, dh, wqkv, cos, sin, dqkv, dqt, away, own, landed, xnt, g2, dx,
    acc_a, acc_b, acc_c, acc_d, land_a, land_b, land_c, land_d, fin_a, fin_b, fin_c, fin_d,
    in_sem, kv_send, kv_recv, dx_send, dx_recv, send_a, recv_a, send_b, recv_b, send_c, recv_c, send_d, recv_d, own_sem,
):
    doc, seq = lax.axis_index("doc"), lax.axis_index("seq")
    core = doc % 2
    ex = Exchange(doc, seq, n_seq)
    tokens, width = xs.shape
    rows = tokens // 2
    pairs = width // LANES

    loads = [
        pltpu.make_async_copy(s, d, in_sem.at[i])
        for i, (s, d) in enumerate(
            [(q_in, q), (k_in, k), (v_in, v), (do_in, do), (lse_in, lse), (dd_in, dd), (xn_in, xn), (x_in, xs), (dh_in, dh), (wqkv_in, wqkv)]
            + [(t.at[pl.ds(core * tokens, tokens)], d) for t, d in ((cos_in, cos), (sin_in, sin))]
        )
    ]
    for load in loads:
        load.start()

    doc_weights = [1 << i for i in range(1, log2(n_doc))]
    seq_weights = [1 << i for i in range(log2(n_seq))]
    sibling = (flipped(doc, 1), seq)
    greet(group_partners(doc, seq, n_seq) + [(flipped(doc, w), seq) for w in doc_weights])

    def reduction(src, lanes, part_width, acc, landing, final, sems, turn, out):
        order = doc_weights[turn:] + doc_weights[:turn]
        partners = [sibling] + [(flipped(doc, w), seq) for w in order] + [(doc, flipped(seq, w)) for w in seq_weights]
        weights = [core] + [bit_of(doc, w) for w in order] + [bit_of(seq, w) for w in seq_weights]
        return Reduction(width, src, lanes, part_width, acc, landing, final, sems, partners, weights, out)

    half1, half2 = g1_in.shape[1] // 2, g2.shape[1] // 2
    wa, wc = acc_a.shape[1], acc_c.shape[1]
    red_a = reduction(g1_in, (0, half1), wa, acc_a, land_a, fin_a, (send_a, recv_a, own_sem.at[0]), 0, g1_o)
    red_b = reduction(g1_in, (wa, half1), half1 - wa, acc_b, land_b, fin_b, (send_b, recv_b, own_sem.at[1]), 1, g1_o)
    red_c = reduction(g2, (0, half2), wc, acc_c, land_c, fin_c, (send_c, recv_c, own_sem.at[2]), 0, g2_o)
    red_d = reduction(g2, (wc, half2), half2 - wc, acc_d, land_d, fin_d, (send_d, recv_d, own_sem.at[3]), 1, g2_o)
    first = list(zip(red_a.steps(), red_b.steps()))
    second = list(zip(red_c.steps(), red_d.steps()))
    progress = [0, 0]

    def advance(which):
        for step in (first, second)[which][progress[which]]:
            step()
        progress[which] += 1

    red_a.start()
    red_b.start()
    for load in loads:
        load.wait()

    def attend_back(keys, j, store_k, store_v, accumulate):
        lanes = pl.ds(pl.multiple_of(j * LANES, LANES), LANES)
        q2, do2 = q[:, lanes], do[:, lanes]
        k2, v2 = k[keys, lanes], v[keys, lanes]
        kt = k2.T
        dks, dvs, dqs = [], [], []
        for sub in range(2):
            probs = jnp.exp(nt(one_head(k2, sub), q2) - lse[j, sub : sub + 1, :])
            dprobs = nt(one_head(v2, sub), do2)
            dscores = (probs * (dprobs - dd[j, sub : sub + 1, :])).astype(BF16)
            dvs.append(nn(probs.astype(BF16), do2))
            dks.append(nn(dscores, q2))
            dqs.append(nn(kt[sub * HEAD_DIM : (sub + 1) * HEAD_DIM], dscores))
        low = lane_of(dks[0].shape) < HEAD_DIM
        store_k(j, lanes, jnp.where(low, dks[0], dks[1]))
        store_v(j, lanes, jnp.where(low, dvs[0], dvs[1]))
        accumulate(j, lanes, jnp.concatenate(dqs, axis=0))

    def unrope(tile):
        return (tile * cos[...] - turned(tile) * sin[...]).astype(BF16)

    def far(j, _):
        def store_k(j, lanes, tile):
            away[0, :, lanes] = tile.astype(BF16)

        def store_v(j, lanes, tile):
            away[1, :, lanes] = tile.astype(BF16)

        def accumulate(j, lanes, tile):
            dqt[j] = tile

        attend_back(pl.ds(tokens, tokens), j, store_k, store_v, accumulate)
        return 0

    def near(j, _):
        def store_k(j, lanes, tile):
            own[0, :, lanes] = tile

        def store_v(j, lanes, tile):
            own[1, :, lanes] = tile

        def accumulate(j, lanes, tile):
            dqkv[:, lanes] = unrope((dqt[j] + tile).T * 0.125)

        attend_back(pl.ds(0, tokens), j, store_k, store_v, accumulate)
        return 0

    lax.fori_loop(0, 4, far, 0)
    advance(0)
    lax.fori_loop(4, pairs, far, 0)
    sends = [
        pltpu.make_async_remote_copy(
            src_ref=away.at[i], dst_ref=landed.at[i], send_sem=kv_send.at[i], recv_sem=kv_recv.at[i],
            device_id=sibling, device_id_type=MESH,
        )
        for i in range(2)
    ]
    for send in sends:
        send.start()
    lax.fori_loop(0, pairs, near, 0)
    for send in sends:
        send.wait()

    def join(j, _):
        lanes = pl.ds(pl.multiple_of(j * LANES, LANES), LANES)
        k_lanes = pl.ds(pl.multiple_of(width + j * LANES, LANES), LANES)
        v_lanes = pl.ds(pl.multiple_of(2 * width + j * LANES, LANES), LANES)
        dqkv[:, k_lanes] = unrope(own[0, :, lanes] + landed[0, :, lanes].astype(F32))
        dqkv[:, v_lanes] = (own[1, :, lanes] + landed[1, :, lanes].astype(F32)).astype(BF16)
        return 0

    lax.fori_loop(0, pairs, join, 0)
    advance(0)
    xnt[...] = xn[...].T
    step = 3 * LANES

    def grad_qkv(j, _):
        lanes = pl.ds(pl.multiple_of(j * step, LANES), step)
        g2[:, lanes] = nn(xnt[...], dqkv[:, lanes]).astype(BF16)
        return 0

    lax.fori_loop(0, 3 * width // step, grad_qkv, 0)
    red_c.start()
    red_d.start()
    grad1 = nt(dqkv[...], wqkv[...])
    unit, scale = row_stats(xs[...].astype(F32))
    dx[...] = (dh[...] + norm_back(grad1, unit, scale, gain1[...])).astype(BF16)
    for slot in range(2):
        send_or_keep(
            ex, ex.back_targets[slot], dx.at[pl.ds(slot * rows, rows)],
            dx_o.at[ex.back_block], dx_send.at[slot], dx_recv.at[ex.back_block],
        )
    advance(0)
    advance(1)
    while progress[0] < len(first) or progress[1] < len(second):
        if progress[0] < len(first):
            advance(0)
        if progress[1] < len(second):
            advance(1)
    for block in range(2):
        wait_bytes(dx_o.at[block], dx_recv.at[block])
    for slot in range(2):
        wait_sent(
            ex, ex.back_targets[slot], dx.at[pl.ds(slot * rows, rows)],
            dx_o.at[ex.back_block], dx_send.at[slot], dx_recv.at[ex.back_block],
        )


def back(n_doc, n_seq, shape, x, xn, q, k, v, do, lse, dd, dh, g1, wqkv, gain1, cos, sin):
    tokens, width = x.shape
    pairs = width // LANES
    cols1, cols2 = g1.shape[1], 3 * width
    rounds = log2(n_doc) - 1 + log2(n_seq)
    tall = Reduction.landing_rows(width, rounds)
    wa = cols1 // 2 // LANES // 2 * LANES
    wb = cols1 // 2 - wa
    wc = cols2 // 2 // LANES // 2 * LANES
    wd = cols2 // 2 - wc
    hbm, vmem = pl.BlockSpec(memory_space=pl.ANY), pl.BlockSpec(memory_space=pltpu.VMEM)
    sds = jax.ShapeDtypeStruct
    rounds_sem = pltpu.SemaphoreType.DMA((2 + 2 * rounds,))
    return pl.pallas_call(
        functools.partial(back_kernel, n_doc, n_seq),
        out_shape=[sds(shape, BF16), sds((width, cols1), BF16), sds((width, cols2), BF16)],
        in_specs=[hbm] * 11 + [vmem] + [hbm] * 2,
        out_specs=[hbm] * 3,
        scratch_shapes=[
            pltpu.VMEM((tokens, width), BF16), pltpu.VMEM((tokens, width), BF16), pltpu.VMEM((tokens, width), BF16),
            pltpu.VMEM((2 * tokens, width), BF16), pltpu.VMEM((2 * tokens, width), BF16), pltpu.VMEM((tokens, width), BF16),
            pltpu.VMEM((pairs, 2, tokens), F32), pltpu.VMEM((pairs, 2, tokens), F32), pltpu.VMEM((tokens, width), F32),
            pltpu.VMEM((width, cols2), BF16), pltpu.VMEM((tokens, LANES), F32), pltpu.VMEM((tokens, LANES), F32),
            pltpu.VMEM((tokens, cols2), BF16), pltpu.VMEM((pairs, LANES, tokens), F32),
            pltpu.VMEM((2, tokens, width), BF16), pltpu.VMEM((2, tokens, width), F32), pltpu.VMEM((2, tokens, width), BF16),
            pltpu.VMEM((width, tokens), BF16), pltpu.VMEM((width, cols2), BF16), pltpu.VMEM((tokens, width), BF16),
        ]
        + [pltpu.VMEM((width, w), BF16) for w in (wa, wb, wc, wd)]
        + [pltpu.VMEM((tall, w), BF16) for w in (wa, wb, wc, wd)]
        + [pltpu.VMEM((width, w), BF16) for w in (wa, wb, wc, wd)]
        + [pltpu.SemaphoreType.DMA((12,))]
        + [pltpu.SemaphoreType.DMA((2,))] * 4
        + [rounds_sem] * 8
        + [pltpu.SemaphoreType.DMA((4,))],
        compiler_params=pltpu.CompilerParams(collective_id=1, has_side_effects=True, vmem_limit_bytes=VMEM_LIMIT),
        name="back",
    )(x, xn, q, k, v, do, lse, dd, dh, g1, wqkv, gain1, cos, sin)


def widen_kernel(ff, g1, g2, wqkv, gain1, dqkv_o, dwo_o, dwin_o, dwout_o, gain1_o, gain2_o):
    width = g1.shape[1] - 3 * ff - LANES
    dwout_o[...] = g1[:, :ff].astype(F32).T
    dwin_o[...] = g1[:, ff : 3 * ff].astype(F32)
    dwo_o[...] = g1[:, 3 * ff : 3 * ff + width].astype(F32)
    gain2_o[...] = g1[:, 3 * ff + width :].astype(F32).T[:8]
    dqkv = g2[...].astype(F32)
    dqkv_o[...] = dqkv
    along = jnp.sum(dqkv * wqkv[...].astype(F32), axis=1, keepdims=True)
    gain1_o[...] = jnp.broadcast_to(along, (LANES, LANES)).T[:8] / gain1[...]


def widen(ff, g1, g2, wqkv, gain1):
    width, cols1 = g1.shape
    cols2 = g2.shape[1]
    sds = jax.ShapeDtypeStruct
    across = lambda i: (i, 0)
    down = lambda i: (0, i)
    return pl.pallas_call(
        functools.partial(widen_kernel, ff),
        grid=(width // LANES,),
        out_shape=[
            sds((width, cols2), F32), sds((width, width), F32), sds((width, 2 * ff), F32), sds((ff, width), F32),
            sds((8, width), F32), sds((8, width), F32),
        ],
        in_specs=[
            pl.BlockSpec((LANES, cols1), across), pl.BlockSpec((LANES, cols2), across),
            pl.BlockSpec((LANES, cols2), across), pl.BlockSpec((1, LANES), down),
        ],
        out_specs=[
            pl.BlockSpec((LANES, cols2), across), pl.BlockSpec((LANES, width), across),
            pl.BlockSpec((LANES, 2 * ff), across), pl.BlockSpec((ff, LANES), down),
            pl.BlockSpec((8, LANES), down), pl.BlockSpec((8, LANES), down),
        ],
        compiler_params=pltpu.CompilerParams(vmem_limit_bytes=VMEM_LIMIT),
        name="widen",
    )(g1, g2, wqkv, gain1)


def rotary_tables(length):
    half = HEAD_DIM // 2
    frequency = ROPE_THETA ** (-(np.arange(half) * 2.0) / HEAD_DIM)
    angles = np.arange(length)[:, None] * frequency[None, :]
    cos, sin = np.cos(angles), np.sin(angles)
    per_tile = LANES // HEAD_DIM
    cos = np.tile(np.concatenate([cos, cos], axis=1), (1, per_tile))
    sin = np.tile(np.concatenate([-sin, sin], axis=1), (1, per_tile))
    return jnp.asarray(cos, F32), jnp.asarray(sin, F32)


def per_device(
    n_doc, n_seq,
    inputs, attn_gain, qkv_weight, attn_out_weight, mlp_gain, mlp_in_weight, mlp_out_weight, cotangent,
):
    blocks, rows, width = inputs.shape
    ff = mlp_out_weight.shape[0]
    cos, sin = rotary_tables(rows * n_seq)
    gain1, gain2 = attn_gain[None], mlp_gain[None]
    output, x, xn, q, k, v, do, lse, dd, dh, g1 = front(
        n_seq, inputs, cotangent, gain1, gain2, qkv_weight, attn_out_weight, mlp_in_weight, mlp_out_weight, cos, sin
    )
    dx, g1, g2 = back(
        n_doc, n_seq, inputs.shape, x, xn, q, k, v, do, lse, dd, dh, g1, qkv_weight, gain1, cos, sin
    )
    dqkv, dwo, dwin, dwout, dgain1, dgain2 = widen(ff, g1, g2, qkv_weight, gain1)
    return output, dx, dgain1[0], dqkv, dwo, dgain2[0], dwin, dwout


def solution(mesh):
    n_doc, n_seq = mesh.shape["doc"], mesh.shape["seq"]
    placed = (P("doc", "seq", None), P(), P(), P(), P(), P(), P(), P("doc", "seq", None))
    return jax.shard_map(
        functools.partial(per_device, n_doc, n_seq),
        mesh=mesh,
        in_specs=placed,
        out_specs=(P("doc", "seq", None), P("doc", "seq", None), P(), P(), P(), P(), P(), P()),
        check_vma=False,
    )
```

time: 752 us -> 238 us (0.32); the launches traced: 744 us -> 238 us
  waiting for transfers between devices: 364 us -> 0 us
  Pallas kernels: 0 us -> 231 us
  local copies, waits for them, and re-layouts: 133 us -> 5.67 us
  matrix products: 77.7 us -> 0 us
  blocking collectives: 72.6 us -> 0 us
  other arithmetic: 49.6 us -> 0 us
  starting transfers between devices: 31.3 us -> 0 us
  between operations: 14.9 us -> 0.67 us
    psum x1 -> x0, waiting for transfers between devices: 268 us -> none  [per_device(): lax.psum((grad_attn_gain, grad_qkv, grad_attn_out, grad_mlp_gain, grad_ml...]
    pallas_call x0 -> x3, Pallas kernels: none -> 231 us  [the longest x1 154 us: back(): pl.pallas_call(functools.partial(back_kernel, n_doc, n_seq), out_shape=[s...]
    all_to_all x7 -> x0, waiting for transfers between devices: 95.5 us -> none  [the longest x1 23.1 us: per_device(): lax.all_to_all(grad_head_v, 'seq', split_axis=1, concat_axis=2, tiled=True)]
    dot_general x30 -> x0, matrix products: 77.7 us -> none  [the longest x2 8.27 us: attend_backward(): jnp.einsum('hqk,khd->qhd', grad_scores, key_heads, preferred_element_type...]
    psum x1 -> x0, blocking collectives: 43.1 us -> none  [per_device(): lax.psum((grad_attn_gain, grad_qkv, grad_attn_out, grad_mlp_gain, grad_ml...]
    all_to_all x7 -> x0, starting transfers between devices: 30.9 us -> none  [the longest x1 6.32 us: per_device(): lax.all_to_all(value_rows, 'seq', split_axis=2, concat_axis=1, tiled=True)]
    all_to_all x12 -> x0, local copies, waits for them, and re-layouts: 29.8 us -> none  [the longest x1 5.84 us: per_device(): lax.all_to_all(mixed_heads, 'seq', split_axis=1, concat_axis=2, tiled=True)]
    all_to_all x1 -> x0, blocking collectives: 29.5 us -> none  [per_device(): lax.all_to_all(mixed_heads, 'seq', split_axis=1, concat_axis=2, tiled=True)]
  transfers between devices with their start and end apart: 8 -> 0, of which waited for: 6 -> 0; matrix products, arithmetic and copies ran while one was open for 12% -> 0% of each run, Pallas kernels for 0% -> 0%
where the time goes in v1:
time: 238 us
  Pallas kernels  231 us (97%)
  local copies, waits for them, and re-layouts  5.67 us (2%)
    pallas_call x1, Pallas kernels, back(): pl.pallas_call(functools.partial(back_kernel, n_doc, n_seq), out_shape=[s...  154 us
    pallas_call x1, Pallas kernels, front(): pl.pallas_call(functools.partial(front_kernel, n_seq), out_shape=[sds((bl...  65.2 us
    pallas_call x1, Pallas kernels, widen(): pl.pallas_call(functools.partial(widen_kernel, ff), grid=(width // LANES,...  12.3 us

profile of v1, /device:TPU:0, one launch (start us, length us, event | category | flops | bytes accessed | tf_op | source)
XLA Modules:
  0.0 237.6 jit_solution(4600475147609015871)
XLA Ops:
  0.6 1.3 broadcast_in_dim.6.gain1
  1.9 1.3 broadcast_in_dim.7.gain2
  3.2 65.2 %front.1 = (bf16[2,256,768]{2,1,0:T(8,128)(2,1)}, bf16[512,768]{1,0:T(8,128)(2,1)}, bf16[512,768]{1,0:T(8,128)(2,1)}, bf16[512,768]{1,0:T(8,128)(2,1)}, bf16[102...) custom-call(bf16[2,256,768]{2,1,0:T(8,128)(2,1)} %x_in.1, ...), custom_call_target="tpu_custom_call" | custom-call | tf_op jit(solution)/shard_map/front/pallas_call | solution.py:336
  68.4 153.8 %back.1 = (bf16[2,256,768]{2,1,0:T(8,128)(2,1)}, bf16[768,4352]{1,0:T(8,128)(2,1)}, bf16[768,2304]{1,0:T(8,128)(2,1)}) custom-call(bf16[512,768]{1,0:T(8,128)(2,1)} %get-tuple-element.29.x_in, bf16[512,768]{1,0:T(8,128)(2,1)} %get-tuple-element.30.xn_in, bf16[512,768]{1,0:T(8,128)(2,1)} %get-tuple-element.31.q_in, bf16[1024,768]{1,0:T(8,128)(2,1)} %get-tuple-element.32.k_in, ...), custom_call_target="tpu_custom_call" | custom-call | tf_op jit(solution)/shard_map/back/pallas_call | solution.py:679
  222.1 0.0 copy-start
  222.1 0.0 copy-start.1
  222.2 12.3 %widen.1 = (f32[768,2304]{1,0:T(8,128)}, f32[768,768]{1,0:T(8,128)}, f32[768,2304]{1,0:T(8,128)}, f32[1152,768]{1,0:T(8,128)}, f32[8,768]{1,0:T(8,128)}, /*index=5*/f32[8,768]{1,0:T(8,128)}) custom-call(bf16[768,4352]{1,0:T(8,128)(2,1)} %get-tuple-element.40.g1, bf16[768,2304]{1,0:T(8,128)(2,1)} %get-tuple-element.41.g2, bf16[768,2304]{1,0:T(8,128)(2,1)} %wqkv.1, ...), custom_call_target="tpu_custom_call" | custom-call | tf_op jit(solution)/shard_map/widen/pallas_call | solution.py:723
  234.5 1.4 slice_reduce_fusion
  235.8 0.0 copy-done
  235.8 0.9 copy.20
  236.7 0.0 copy-done.1
  236.7 0.9 copy.21
Async XLA Ops:
  222.1 13.7 %copy-start = (bf16[2,256,768]{2,1,0:T(8,128)(2,1)S(1)}, bf16[2,256,768]{2,1,0:T(8,128)(2,1)}, u32[]{:S(2)}) copy-start(bf16[2,256,768]{2,1,0:T(8,128)(2,1)} %get-tuple-element.58) | copy-start | bytes 2359300
  222.1 14.6 %copy-start.1 = (bf16[2,256,768]{2,1,0:T(8,128)(2,1)S(1)}, bf16[2,256,768]{2,1,0:T(8,128)(2,1)}, u32[]{:S(2)}) copy-start(bf16[2,256,768]{2,1,0:T(8,128)(2,1)} %get-tuple-element.59) | copy-start | bytes 2359300

commit v2 on v1

v2 whole, which is shorter than its diff:
```python
import functools

import jax
import jax.numpy as jnp
import numpy as np
from jax import lax
from jax.experimental import pallas as pl
from jax.experimental.pallas import tpu as pltpu
from jax.sharding import PartitionSpec as P

HEAD_DIM = 64
ROPE_THETA = 160000.0
NORM_EPSILON = 1e-05
F32 = jnp.float32
BF16 = jnp.bfloat16
MESH = pl.DeviceIdType.MESH
LANES = 128
VMEM_LIMIT = 60 << 20


def nn(a, b):
    return lax.dot_general(a, b, (((1,), (0,)), ((), ())), preferred_element_type=F32)


def nt(a, b):
    return lax.dot_general(a, b, (((1,), (1,)), ((), ())), preferred_element_type=F32)


def lane_of(shape):
    return lax.broadcasted_iota(jnp.int32, shape, 1)


def one_head(pair, sub):
    lane = lane_of(pair.shape)
    mine = (lane < HEAD_DIM) if sub == 0 else (lane >= HEAD_DIM)
    return jnp.where(mine, pair, jnp.zeros_like(pair))


def turned(values):
    back = pltpu.roll(values, HEAD_DIM // 2, 1)
    ahead = pltpu.roll(values, LANES - HEAD_DIM // 2, 1)
    return jnp.where(lane_of(values.shape) % HEAD_DIM < HEAD_DIM // 2, ahead, back)


def row_stats(values):
    mean = jnp.mean(values, axis=1, keepdims=True)
    centered = values - mean
    scale = lax.rsqrt(jnp.mean(centered * centered, axis=1, keepdims=True) + NORM_EPSILON)
    return centered * scale, scale


def norm_back(grad, unit, scale, gain):
    weighted = grad * gain
    along = jnp.mean(weighted, axis=1, keepdims=True)
    across = jnp.mean(weighted * unit, axis=1, keepdims=True)
    return scale * (weighted - along - unit * across)


def bit_of(index, weight):
    return (index // weight) % 2


def flipped(index, weight):
    return index + weight - 2 * weight * bit_of(index, weight)


def greet(partners):
    barrier = pltpu.get_barrier_semaphore()
    for partner in partners:
        pl.semaphore_signal(barrier, inc=1, device_id=partner, device_id_type=MESH)
    pl.semaphore_wait(barrier, len(partners))


def group_partners(doc, seq, n_seq):
    core = doc % 2
    found = []
    for other_core in range(2):
        for step in range(n_seq):
            if other_core == 0 and step == 0:
                continue
            found.append(
                (doc - core + (core + other_core) % 2, (seq + step) % n_seq)
            )
    return found


class Exchange:
    def __init__(self, doc, seq, n_seq):
        core = doc % 2
        half = n_seq // 2
        base = doc - core
        self.out_targets = [(base + seq // half, 2 * core + block) for block in range(2)]
        self.out_slot = seq % half
        self.back_targets = [(base + seq // 2, half * core + slot) for slot in range(2)]
        self.back_block = seq % 2
        self.doc, self.seq = doc, seq

    def is_self(self, target):
        return jnp.logical_and(target[0] == self.doc, target[1] == self.seq)


def send_or_keep(ex, target, src, dst, send_sem, recv_sem):
    mine = ex.is_self(target)

    @pl.when(mine)
    def _():
        pltpu.make_async_copy(src, dst, recv_sem).start()

    @pl.when(jnp.logical_not(mine))
    def _():
        pltpu.make_async_remote_copy(
            src_ref=src, dst_ref=dst, send_sem=send_sem, recv_sem=recv_sem,
            device_id=target, device_id_type=MESH,
        ).start()


def wait_sent(ex, target, src, dst, send_sem, recv_sem):
    @pl.when(jnp.logical_not(ex.is_self(target)))
    def _():
        pltpu.make_async_remote_copy(
            src_ref=src, dst_ref=dst, send_sem=send_sem, recv_sem=recv_sem,
            device_id=target, device_id_type=MESH,
        ).wait_send()


def wait_bytes(ref, sem):
    pltpu.make_async_copy(ref, ref, sem).wait()


LINK_RATE, CORE_RATE, ROUND_LATENCY = 44e3, 500e3, 2.5
STEP_TIME, ADD_TIME = 0.1, 0.4e-6
PIECE_TIME = {"feed": 1.1, "mix": 1.8, "norm": 2.8, "wo": 1.5, "do": 2.0, "far": 1.25, "near": 1.25, "join": 1.8, "dx": 2.2}
FEED_GROUPS = ((0, 2), (2, 4), (4, 6), (6, 8))
FIRST_PAIRS = 4


def log2(n):
    return n.bit_length() - 1


class Stream:
    def __init__(self, first, second, count):
        self.first, self.second, self.count = first, second, count


def halvings(rows, rounds):
    kept, extent = [], rows
    for _ in range(rounds):
        split = (extent // 2) % 16 == 0
        extent = extent // 2 if split else extent
        kept.append((extent, split))
    return kept


def axes_of(n_doc, n_seq):
    doc_axes = [("doc", 1 << i) for i in range(1, log2(n_doc))]
    seq_axes = [("seq", 1 << i) for i in range(log2(n_seq))]
    return doc_axes, seq_axes


def axis_order(index, n_doc, n_seq):
    doc_axes, seq_axes = axes_of(n_doc, n_seq)
    turn = (0, 1, 0, 0, 1, 1)[index % 6] * (len(doc_axes) // 2)
    doc_axes = doc_axes[turn:] + doc_axes[:turn]
    near, far = seq_axes[:-1], seq_axes[-1:]
    return (near + doc_axes if index % 3 == 2 else doc_axes + near) + far


def stream_plan(width, ff):
    ffs, pairs = ff // LANES, width // LANES
    streams, ready = [], {}

    def add(piece, first, second, count):
        ready.setdefault(piece, []).append(len(streams))
        streams.append(Stream(first, second, count))

    for low, high in FEED_GROUPS:
        count = (high - low) // 2
        for base in (0, ffs, 2 * ffs):
            add(("feed", high - 1), base + low, base + low + count, count)
    covered = FEED_GROUPS[-1][1]
    assert ffs - covered == 1 and pairs % 2 == 0
    add(("feed", ffs - 1), covered, ffs + covered, 1)
    add(("norm", 0), 2 * ffs + covered, 3 * ffs + pairs, 1)
    half = pairs // 2
    add(("wo", 0), 3 * ffs, 3 * ffs + half, half)
    base = 3 * ffs + pairs + 1
    for part, (low, high) in enumerate(((0, FIRST_PAIRS), (FIRST_PAIRS, pairs))):
        for third in range(3):
            start, count = base + third * pairs + low, (high - low) // 2
            add(("join", part), start, start + count, count)
    return streams, ready, base + 3 * pairs


def piece_list(ff, pairs):
    ffs = ff // LANES
    pieces = [("feed", j) for j in range(ffs)]
    pieces += [("mix", 0), ("norm", 0), ("wo", 0), ("do", 0)]
    for part, (low, high) in enumerate(((0, FIRST_PAIRS), (FIRST_PAIRS, pairs))):
        pieces += [("far", j) for j in range(low, high)] + [("near", j) for j in range(low, high)]
        pieces.append(("join", part))
    return pieces + [("dx", 0)]


def agenda(streams, ready, pieces, rows, n_doc, n_seq):
    rounds = log2(n_doc) - 1 + log2(n_seq)
    kept = halvings(rows, rounds)
    ups = [r for r in reversed(range(rounds)) if kept[r][1]]
    free, flying, steps = {}, [], {}
    near, far = axes_of(n_doc, n_seq)[1]

    def legs(index):
        order = axis_order(index, n_doc, n_seq)
        unit = streams[index].count * LANES * 2
        trip = [("core", rows * unit)]
        trip += [(order[r], kept[r][0] * unit) for r in range(rounds)]
        trip += [(order[r], kept[r][0] * unit) for r in ups]
        return trip + [("core", rows * unit)]

    def occupy(axis, size, when):
        rate = CORE_RATE if axis == "core" else LINK_RATE / 2 if axis == far else LINK_RATE
        begin = max(when, free.get(axis, 0.0))
        free[axis] = begin + size / rate
        if axis == far:
            free[near] = max(free.get(near, 0.0), begin) + 0.5 * size / LINK_RATE
        return free[axis]

    def depart(index, leg, when):
        flying.append((occupy(*legs(index)[leg], when) + ROUND_LATENCY, index, leg))

    def serve(now):
        flying.sort()
        done, index, leg = flying.pop(0)
        trip = legs(index)
        now = max(now, done) + STEP_TIME + (trip[leg][1] * ADD_TIME if leg <= rounds else 0.0)
        if leg + 1 < len(trip):
            depart(index, leg + 1, now)
        return now, (index, leg)

    now = 0.0
    for piece in pieces:
        now += PIECE_TIME[piece[0]]
        actions = steps.setdefault(piece, [])
        if piece[0] in ("mix", "dx"):
            occupy(far, 393e3, now)
            occupy(near, 200e3, now)
        for index in ready.get(piece, ()):
            actions.append((index, -1))
            depart(index, 0, now)
            now += STEP_TIME
        while flying and min(flying)[0] <= now:
            now, action = serve(now)
            actions.append(action)
    last = steps.setdefault("end", [])
    while flying:
        now, action = serve(now)
        last.append(action)
    return steps


class Reducer:
    def __init__(self, streams, n_doc, n_seq, doc, seq, grads, landing, final, out, send_sem, recv_sem, own_sem):
        self.streams, self.grads, self.landing, self.final, self.out = streams, grads, landing, final, out
        self.send_sem, self.recv_sem, self.own_sem = send_sem, recv_sem, own_sem
        self.core = doc % 2
        self.rows = grads.shape[1]
        self.rounds = log2(n_doc) - 1 + log2(n_seq)
        self.kept = halvings(self.rows, self.rounds)
        self.ups = [r for r in reversed(range(self.rounds)) if self.kept[r][1]]
        self.legs = 2 + self.rounds + len(self.ups)
        self.sibling = (flipped(doc, 1), seq)
        self.bits, self.partners = {}, {}
        for name, weight in sum(axes_of(n_doc, n_seq), []):
            index = doc if name == "doc" else seq
            self.bits[name, weight] = bit_of(index, weight)
            self.partners[name, weight] = (flipped(doc, weight), seq) if name == "doc" else (doc, flipped(seq, weight))
        self.orders = [axis_order(i, n_doc, n_seq) for i in range(len(streams))]
        self.slots, used = [], 0
        for stream in streams:
            self.slots.append(pl.ds(used, stream.count))
            used += stream.count
        self.plans = []
        for order in self.orders:
            offset, base, plan = 0, 0, []
            for (keep, split), axis in zip(self.kept, order):
                bit = self.bits[axis]
                mine = offset + bit * keep if split else offset
                theirs = offset + (1 - bit) * keep if split else offset
                plan.append((mine, theirs, base, keep))
                base += keep
                offset = mine
            self.plans.append(plan)

    @staticmethod
    def landing_rows(rows, rounds):
        return sum(keep for keep, _ in halvings(rows, rounds))

    def tiles(self, index, other=False):
        stream = self.streams[index]
        side = 1 - self.core if other else self.core
        return pl.ds(stream.first + side * (stream.second - stream.first), stream.count)

    def span(self, start, extent):
        return pl.ds(start if isinstance(start, int) else pl.multiple_of(start, 16), extent)

    def copy(self, index, leg, receiving=False):
        slot = self.slots[index]
        if leg == 0:
            src, dst, partner = self.grads.at[self.tiles(index, True)], self.final.at[slot], self.sibling
        elif leg <= self.rounds:
            mine, theirs, base, keep = self.plans[index][leg - 1]
            src = self.grads.at[self.tiles(index), self.span(theirs, keep)]
            dst, partner = self.landing.at[slot, pl.ds(base, keep)], self.partners[self.orders[index][leg - 1]]
        elif leg < self.legs - 1:
            r = self.ups[leg - 1 - self.rounds]
            mine, theirs, base, keep = self.plans[index][r]
            src = dst = self.final.at[slot, self.span(theirs if receiving else mine, keep)]
            partner = self.partners[self.orders[index][r]]
        else:
            src, dst, partner = self.final.at[slot], self.out.at[self.tiles(index, receiving)], self.sibling
        return pltpu.make_async_remote_copy(
            src_ref=src, dst_ref=dst, send_sem=self.send_sem.at[index, leg], recv_sem=self.recv_sem.at[index, leg],
            device_id=partner, device_id_type=MESH,
        )

    def own(self, index):
        return pltpu.make_async_copy(self.final.at[self.slots[index]], self.out.at[self.tiles(index)], self.own_sem.at[index])

    def add(self, index, leg):
        stream, slot = self.streams[index], self.slots[index]
        start = stream.first + self.core * (stream.second - stream.first)
        low = slot.start
        if leg == 0:
            mine, base, keep = 0, 0, self.rows
        else:
            mine, _, base, keep = self.plans[index][leg - 1]
        block = keep
        while block > 96:
            block //= 2

        def body(i, _):
            here = self.span(mine + i * block, block)
            for t in range(stream.count):
                if leg == 0:
                    other = self.final[low + t, here]
                else:
                    other = self.landing[low + t, self.span(base + i * block, block)]
                total = (self.grads[start + t, here].astype(F32) + other.astype(F32)).astype(BF16)
                if leg == self.rounds:
                    self.final[low + t, here] = total
                else:
                    self.grads[start + t, here] = total
            return 0

        lax.fori_loop(0, keep // block, body, 0)

    def act(self, index, leg):
        if leg >= 0:
            self.copy(index, leg).wait_send()
            self.copy(index, leg, True).wait_recv()
            if leg <= self.rounds:
                self.add(index, leg)
            if leg == self.legs - 1:
                self.own(index).wait()
        if leg + 1 < self.legs:
            self.copy(index, leg + 1).start()
        if leg + 1 == self.legs - 1:
            self.own(index).start()


def layer_kernel(
    n_doc, n_seq,
    x_in, cot_in, gain1_in, gain2_in, wqkv_in, wo_in, win_in, wout_in, cos_in, sin_in,
    out_o, dx_o, g_o,
    xs, cs, outs, wqkv, wo, win, wout, cos, sin, xn, q, k, v, att, h, xn2, xn2t, hid, dgu, dmt, do, dh, acc, lse, dd,
    dqt, landed, grads, landing, final,
    w_sem, send_sem, recv_sem, kv_send, kv_recv, sum_send, sum_recv, own_sem,
):
    doc, seq = lax.axis_index("doc"), lax.axis_index("seq")
    core = doc % 2
    ex = Exchange(doc, seq, n_seq)
    rows = x_in.shape[1]
    tokens, width = xs.shape
    ff = wout.shape[0]
    ffs, pairs = ff // LANES, width // LANES
    sibling = (flipped(doc, 1), seq)

    loads = [
        pltpu.make_async_copy(s, d, w_sem.at[i])
        for i, (s, d) in enumerate(
            [(wqkv_in, wqkv), (wo_in, wo), (win_in, win), (wout_in, wout)]
            + [(t.at[pl.ds(core * tokens, tokens)], d) for t, d in ((cos_in, cos), (sin_in, sin))]
        )
    ]
    greet(group_partners(doc, seq, n_seq) + [(flipped(doc, w), seq) for _, w in axes_of(n_doc, n_seq)[0]])

    def spread(src, dst, base, act):
        for block in range(2):
            act(
                ex, ex.out_targets[block], src.at[block], dst.at[pl.ds(ex.out_slot * rows, rows)],
                send_sem.at[base + block], recv_sem.at[base + ex.out_slot],
            )

    def gather(src, dst, base, act):
        for slot in range(2):
            act(
                ex, ex.back_targets[slot], src.at[pl.ds(slot * rows, rows)], dst.at[ex.back_block],
                send_sem.at[base + slot], recv_sem.at[base + ex.back_block],
            )

    spread(x_in, xs, 0, send_or_keep)
    for load in loads:
        load.start()
    gain1, gain2 = gain1_in[...].reshape(1, width), gain2_in[...].reshape(1, width)

    streams, ready, _ = stream_plan(width, ff)
    steps = agenda(streams, ready, piece_list(ff, pairs), width, n_doc, n_seq)
    reducer = Reducer(streams, n_doc, n_seq, doc, seq, grads, landing, final, g_o, sum_send, sum_recv, own_sem)

    def after(piece):
        for action in steps.get(piece, ()):
            reducer.act(*action)

    def loop(name, low, high, body):
        def one(j, _):
            body(j)
            for at in range(low, high):
                if steps.get((name, at)):
                    pl.when(j == at)(functools.partial(after, (name, at)))
            return 0

        lax.fori_loop(low, high, one, 0)

    def tile(j, base=0, count=1):
        return pl.ds(pl.multiple_of(base + j * LANES * count, LANES), LANES * count)

    for slot in range(2):
        wait_bytes(xs.at[pl.ds(slot * rows, rows)], recv_sem.at[slot])
    spread(cot_in, cs, 2, send_or_keep)

    unit, _ = row_stats(xs[...].astype(F32))
    xn[...] = (unit * gain1).astype(BF16)
    for i in (0, 4, 5):
        loads[i].wait()

    def roped(part, scale):
        return ((part * cos[...] + turned(part) * sin[...]) * scale).astype(BF16)

    def project(j, _):
        weights = jnp.concatenate([wqkv[:, tile(j, width)], wqkv[:, tile(j, 2 * width)]], axis=1)
        both = nn(xn[...], weights)
        k[:tokens, tile(j)] = roped(both[:, :LANES], 1.0)
        v[:tokens, tile(j)] = both[:, LANES:].astype(BF16)
        return 0

    lax.fori_loop(0, pairs, project, 0)
    kv_copies = [
        pltpu.make_async_remote_copy(
            src_ref=ref.at[pl.ds(0, tokens)], dst_ref=ref.at[pl.ds(tokens, tokens)],
            send_sem=kv_send.at[i], recv_sem=kv_recv.at[i], device_id=sibling, device_id_type=MESH,
        )
        for i, ref in enumerate((k, v))
    ]
    for copy in kv_copies:
        copy.start()

    def project_q(j, _):
        both = nn(xn[...], wqkv[:, tile(j, 0, 2)])
        for t in range(2):
            q[:, tile(2 * j + t)] = roped(both[:, t * LANES : (t + 1) * LANES], 0.125)
        return 0

    lax.fori_loop(0, pairs // 2, project_q, 0)
    for copy in kv_copies:
        copy.wait()

    def attend(j, _):
        lanes = tile(j)
        k2, vt, q2 = k[:, lanes], v[:, lanes].T, q[:, lanes]
        mixed = []
        for sub in range(2):
            scores = nt(one_head(k2, sub), q2)
            top = jnp.max(scores, axis=0, keepdims=True)
            weights = jnp.exp(scores - top)
            total = jnp.sum(weights, axis=0, keepdims=True)
            lse[j, sub : sub + 1, :] = top + jnp.log(total)
            mixed.append(
                nn(vt[sub * HEAD_DIM : (sub + 1) * HEAD_DIM], weights.astype(BF16)) * (1.0 / total)
            )
        att[:, lanes] = jnp.concatenate(mixed, axis=0).T.astype(BF16)
        return 0

    lax.fori_loop(0, pairs, attend, 0)

    loads[1].wait()
    h[...] = xs[...].astype(F32) + nn(att[...], wo[...])
    unit2, _ = row_stats(h[...])
    xn2[...] = (unit2 * gain2).astype(BF16)
    xn2t[...] = xn2[...].T
    loads[2].wait()
    loads[3].wait()
    for slot in range(2):
        wait_bytes(cs.at[pl.ds(slot * rows, rows)], recv_sem.at[2 + slot])
    dmt[...] = cs[...].T

    def feed(j):
        both = nn(xn2[...], jnp.concatenate([win[:, tile(j)], win[:, tile(j, ff)]], axis=1))
        gate, up = both[:, :LANES], both[:, LANES:]
        phi = 0.5 * (1.0 + lax.erf(gate * 0.7071067811865476))
        slope = phi + gate * (0.3989422804014327 * jnp.exp(-0.5 * gate * gate))
        active = gate * phi
        inner = (active * up).astype(BF16)
        hid[:, tile(j)] = inner
        dhid = nt(cs[...], wout[tile(j), :])
        dgate, dup = (dhid * up * slope).astype(BF16), (dhid * active).astype(BF16)
        dgu[:, tile(j)] = dgate
        dgu[:, tile(j, ff)] = dup
        grads[j] = nn(dmt[...], inner).astype(BF16)
        pair = nn(xn2t[...], jnp.concatenate([dgate, dup], axis=1)).astype(BF16)
        grads[ffs + j] = pair[:, :LANES]
        grads[2 * ffs + j] = pair[:, LANES:]

    loop("feed", 0, ffs, feed)

    outs[...] = (h[...] + nn(hid[...], wout[...])).astype(BF16)
    gather(outs, out_o, 4, send_or_keep)
    after(("mix", 0))

    acc[...] = nt(dgu[...], win[...])
    unit2, scale2 = row_stats(h[...])
    grad2 = acc[...]
    dh[...] = cs[...].astype(F32) + norm_back(grad2, unit2, scale2, gain2)
    gain_terms = (grad2 * unit2).astype(BF16).T
    grads[3 * ffs + pairs] = nn(gain_terms, jnp.ones((tokens, LANES), BF16)).astype(BF16)
    after(("norm", 0))

    datt = dh[...].astype(BF16)
    att_t = att[...].T
    for j in range(pairs // 2):
        both = nn(att_t, datt[:, 2 * j * LANES : (2 * j + 2) * LANES]).astype(BF16)
        for t in range(2):
            grads[3 * ffs + 2 * j + t] = both[:, t * LANES : (t + 1) * LANES]
    after(("wo", 0))

    do[...] = nt(datt, wo[...]).astype(BF16)
    lane = lax.broadcasted_iota(jnp.int32, (8, LANES), 1)
    row = lax.broadcasted_iota(jnp.int32, (8, LANES), 0)
    pick = jnp.where(lane // HEAD_DIM == row, 1.0, 0.0).astype(F32)
    for j in range(pairs):
        lanes = slice(j * LANES, (j + 1) * LANES)
        product = do[:, lanes].astype(F32) * att[:, lanes].astype(F32)
        sums = lax.dot_general(
            pick, product, (((1,), (1,)), ((), ())),
            precision=lax.Precision.HIGHEST, preferred_element_type=F32,
        )
        dd[j] = sums[:2]
    after(("do", 0))

    dqkv, xnt, dx = win.at[pl.ds(0, tokens)], xn2t, do
    away, own = (xn2, att), (h, acc)
    xnt[...] = xn[...].T

    def attend_back(keys, j):
        lanes = tile(j)
        q2, do2 = q[:, lanes], do[:, lanes]
        k2, v2 = k[keys, lanes], v[keys, lanes]
        kt = k2.T
        dks, dvs, dqs = [], [], []
        for sub in range(2):
            probs = jnp.exp(nt(one_head(k2, sub), q2) - lse[j, sub : sub + 1, :])
            dprobs = nt(one_head(v2, sub), do2)
            dscores = (probs * (dprobs - dd[j, sub : sub + 1, :])).astype(BF16)
            dvs.append(nn(probs.astype(BF16), do2))
            dks.append(nn(dscores, q2))
            dqs.append(nn(kt[sub * HEAD_DIM : (sub + 1) * HEAD_DIM], dscores))
        low = lane_of(dks[0].shape) < HEAD_DIM
        return jnp.where(low, dks[0], dks[1]), jnp.where(low, dvs[0], dvs[1]), jnp.concatenate(dqs, axis=0)

    def unrope(part):
        return (part * cos[...] - turned(part) * sin[...]).astype(BF16)

    def far(j):
        dk, dv, dq = attend_back(pl.ds(tokens, tokens), j)
        away[0][:, tile(j)] = dk.astype(BF16)
        away[1][:, tile(j)] = dv.astype(BF16)
        dqt[j] = dq

    def near(j):
        dk, dv, dq = attend_back(pl.ds(0, tokens), j)
        own[0][:, tile(j)] = dk
        own[1][:, tile(j)] = dv
        dqkv[:, tile(j)] = unrope((dqt[j] + dq).T * 0.125)

    def join(j, _):
        dqkv[:, tile(j, width)] = unrope(own[0][:, tile(j)] + landed[0, :, tile(j)].astype(F32))
        dqkv[:, tile(j, 2 * width)] = (own[1][:, tile(j)] + landed[1, :, tile(j)].astype(F32)).astype(BF16)
        return 0

    base = 3 * ffs + pairs + 1
    for part, (low, high) in enumerate(((0, FIRST_PAIRS), (FIRST_PAIRS, pairs))):
        loop("far", low, high, far)
        lanes = pl.ds(low * LANES, (high - low) * LANES)
        sends = [
            pltpu.make_async_remote_copy(
                src_ref=away[i].at[:, lanes], dst_ref=landed.at[i, :, lanes],
                send_sem=kv_send.at[2 + 2 * part + i], recv_sem=kv_recv.at[2 + 2 * part + i],
                device_id=sibling, device_id_type=MESH,
            )
            for i in range(2)
        ]
        for send in sends:
            send.start()
        loop("near", low, high, near)
        for send in sends:
            send.wait()
        lax.fori_loop(low, high, join, 0)

        def weight_grads(j, _):
            for third in range(3):
                both = nn(xnt[...], dqkv[:, tile(j, third * width, 2)]).astype(BF16)
                for t in range(2):
                    grads[base + third * pairs + 2 * j + t] = both[:, t * LANES : (t + 1) * LANES]
            return 0

        lax.fori_loop(low // 2, high // 2, weight_grads, 0)
        after(("join", part))

    grad1 = nt(dqkv[...], wqkv[...])
    unit, scale = row_stats(xs[...].astype(F32))
    dx[...] = (dh[...] + norm_back(grad1, unit, scale, gain1)).astype(BF16)
    gather(dx, dx_o, 6, send_or_keep)
    after(("dx", 0))
    after("end")

    spread(x_in, xs, 0, wait_sent)
    spread(cot_in, cs, 2, wait_sent)
    gather(outs, out_o, 4, wait_sent)
    gather(dx, dx_o, 6, wait_sent)
    for block in range(2):
        wait_bytes(out_o.at[block], recv_sem.at[4 + block])
        wait_bytes(dx_o.at[block], recv_sem.at[6 + block])


def layer(n_doc, n_seq, inputs, cotangent, gain1, gain2, wqkv, wo, win, wout, cos, sin):
    blocks, rows, width = inputs.shape
    tokens = blocks * rows
    ff = wout.shape[0]
    pairs = width // LANES
    streams, _, total = stream_plan(width, ff)
    rounds = log2(n_doc) - 1 + log2(n_seq)
    kept = halvings(width, rounds)
    legs = 2 + rounds + sum(1 for _, split in kept if split)
    slots = sum(stream.count for stream in streams)
    hbm, vmem = pl.BlockSpec(memory_space=pl.ANY), pl.BlockSpec(memory_space=pltpu.VMEM)
    sds, dma = jax.ShapeDtypeStruct, pltpu.SemaphoreType.DMA
    row_b = pltpu.VMEM((tokens, width), BF16)
    row_f = pltpu.VMEM((tokens, width), F32)
    return pl.pallas_call(
        functools.partial(layer_kernel, n_doc, n_seq),
        out_shape=[
            sds((blocks, rows, width), BF16), sds((blocks, rows, width), BF16), sds((total, width, LANES), BF16),
        ],
        in_specs=[hbm, hbm, vmem, vmem] + [hbm] * 6,
        out_specs=[hbm] * 3,
        scratch_shapes=[
            row_b, row_b, row_b,
            pltpu.VMEM(wqkv.shape, BF16), pltpu.VMEM(wo.shape, BF16), pltpu.VMEM(win.shape, BF16), pltpu.VMEM(wout.shape, BF16),
            pltpu.VMEM((tokens, LANES), F32), pltpu.VMEM((tokens, LANES), F32),
            row_b, row_b, pltpu.VMEM((2 * tokens, width), BF16), pltpu.VMEM((2 * tokens, width), BF16),
            row_b, row_f, row_b, pltpu.VMEM((width, tokens), BF16),
            pltpu.VMEM((tokens, ff), BF16), pltpu.VMEM((tokens, 2 * ff), BF16), pltpu.VMEM((width, tokens), BF16),
            row_b, row_f, row_f,
            pltpu.VMEM((pairs, 2, tokens), F32), pltpu.VMEM((pairs, 2, tokens), F32),
            pltpu.VMEM((pairs, LANES, tokens), F32), pltpu.VMEM((2, tokens, width), BF16),
            pltpu.VMEM((total, width, LANES), BF16),
            pltpu.VMEM((slots, Reducer.landing_rows(width, rounds), LANES), BF16),
            pltpu.VMEM((slots, width, LANES), BF16),
            dma((6,)), dma((8,)), dma((8,)), dma((6,)), dma((6,)),
            dma((len(streams), legs)), dma((len(streams), legs)), dma((len(streams),)),
        ],
        compiler_params=pltpu.CompilerParams(collective_id=0, has_side_effects=True, vmem_limit_bytes=VMEM_LIMIT),
        name="layer",
    )(inputs, cotangent, gain1, gain2, wqkv, wo, win, wout, cos, sin)


def widen_kernel(ff, width, g, wqkv, gain1, dqkv_o, dwo_o, dwin_o, dwout_o, gain1_o, gain2_o):
    ffs, pairs = ff // LANES, width // LANES
    base = 3 * ffs + pairs + 1
    for j in range(ffs):
        dwout_o[j * LANES : (j + 1) * LANES, :] = g[j].astype(F32).T
    for j in range(2 * ffs):
        dwin_o[:, j * LANES : (j + 1) * LANES] = g[ffs + j].astype(F32)
    for j in range(pairs):
        dwo_o[:, j * LANES : (j + 1) * LANES] = g[3 * ffs + j].astype(F32)
    gain2_o[...] = g[base - 1].astype(F32).T[0]
    along = jnp.zeros((LANES, LANES), F32)
    for j in range(3 * pairs):
        lanes = slice(j * LANES, (j + 1) * LANES)
        part = g[base + j].astype(F32)
        dqkv_o[:, lanes] = part
        along += part * wqkv[:, lanes].astype(F32)
    total = jnp.sum(along.T, axis=0, keepdims=True)
    gain1_o[...] = (total / gain1[...].reshape(1, LANES))[0]


def widen(ff, g, wqkv, gain1):
    total, width, _ = g.shape
    sds = jax.ShapeDtypeStruct
    across = lambda i: (i, 0)
    down = lambda i: (0, i)
    flat = pl.BlockSpec((LANES,), lambda i: (i,))
    return pl.pallas_call(
        functools.partial(widen_kernel, ff, width),
        grid=(width // LANES,),
        out_shape=[
            sds(wqkv.shape, F32), sds((width, width), F32), sds((width, 2 * ff), F32), sds((ff, width), F32),
            sds((width,), F32), sds((width,), F32),
        ],
        in_specs=[
            pl.BlockSpec((total, LANES, LANES), lambda i: (0, i, 0)), pl.BlockSpec((LANES, wqkv.shape[1]), across), flat,
        ],
        out_specs=[
            pl.BlockSpec((LANES, wqkv.shape[1]), across), pl.BlockSpec((LANES, width), across),
            pl.BlockSpec((LANES, 2 * ff), across), pl.BlockSpec((ff, LANES), down), flat, flat,
        ],
        compiler_params=pltpu.CompilerParams(vmem_limit_bytes=VMEM_LIMIT),
        name="widen",
    )(g, wqkv, gain1)


def rotary_tables(length):
    half = HEAD_DIM // 2
    frequency = ROPE_THETA ** (-(np.arange(half) * 2.0) / HEAD_DIM)
    angles = np.arange(length)[:, None] * frequency[None, :]
    cos, sin = np.cos(angles), np.sin(angles)
    per_tile = LANES // HEAD_DIM
    cos = np.tile(np.concatenate([cos, cos], axis=1), (1, per_tile))
    sin = np.tile(np.concatenate([-sin, sin], axis=1), (1, per_tile))
    return jnp.asarray(cos, F32), jnp.asarray(sin, F32)


def per_device(
    n_doc, n_seq,
    inputs, attn_gain, qkv_weight, attn_out_weight, mlp_gain, mlp_in_weight, mlp_out_weight, cotangent,
):
    blocks, rows, width = inputs.shape
    ff = mlp_out_weight.shape[0]
    cos, sin = rotary_tables(rows * n_seq)
    output, dx, grads = layer(
        n_doc, n_seq, inputs, cotangent, attn_gain, mlp_gain,
        qkv_weight, attn_out_weight, mlp_in_weight, mlp_out_weight, cos, sin,
    )
    dqkv, dwo, dwin, dwout, dgain1, dgain2 = widen(ff, grads, qkv_weight, attn_gain)
    return output, dx, dgain1, dqkv, dwo, dgain2, dwin, dwout


def solution(mesh):
    n_doc, n_seq = mesh.shape["doc"], mesh.shape["seq"]
    placed = (P("doc", "seq", None), P(), P(), P(), P(), P(), P(), P("doc", "seq", None))
    return jax.shard_map(
        functools.partial(per_device, n_doc, n_seq),
        mesh=mesh,
        in_specs=placed,
        out_specs=(P("doc", "seq", None), P("doc", "seq", None), P(), P(), P(), P(), P(), P()),
        check_vma=False,
    )
```

time: 238 us -> 193 us (0.81)
  Pallas kernels: 231 us -> 190 us
  local copies, waits for them, and re-layouts: 5.67 us -> 1.77 us
    pallas_call x3 -> x2, Pallas kernels: 231 us -> 190 us  [the longest x1 178 us: layer(): pl.pallas_call(functools.partial(layer_kernel, n_doc, n_seq), out_shape=[...]
    broadcast_in_dim x2 -> x0, local copies, waits for them, and re-layouts: 2.53 us -> none  [per_device(): gain1, gain2 = (attn_gain[None], mlp_gain[None])]
where the time goes in v2:
time: 193 us
  Pallas kernels  190 us (98%)
    pallas_call x1, Pallas kernels, layer(): pl.pallas_call(functools.partial(layer_kernel, n_doc, n_seq), out_shape=[...  178 us
    pallas_call x1, Pallas kernels, widen(): pl.pallas_call(functools.partial(widen_kernel, ff, width), grid=(width //...  12.3 us

profile of v2, /device:TPU:0, one launch (start us, length us, event | category | flops | bytes accessed | tf_op | source)
XLA Modules:
  0.0 192.8 jit_solution(4637211351078346496)
XLA Ops:
  0.6 178.0 %layer.1 = (bf16[2,256,768]{2,1,0:T(8,128)(2,1)}, bf16[2,256,768]{2,1,0:T(8,128)(2,1)}, bf16[52,768,128]{2,1,0:T(8,128)(2,1)}) custom-call(bf16[2,256,768]{2,1,0:T(8,128)(2,1)} %x_in.1, bf16[2,256,768]{2,1,0:T(8,128)(2,1)} %cot_in.1, f32[768]{0:T(1024)} %gain1.1, f32[768]{0:T(1024)} %gain2_in.1, bf16[768,2304]{1,0:T(8,128)(2,1)} %wqkv.1, ...), custom_call_target="tpu_custom_call" | custom-call | tf_op jit(solution)/shard_map/layer/pallas_call | solution.py:658
  178.7 0.0 copy-start.1
  178.7 0.0 copy-start
  178.7 12.3 %widen.1 = (f32[768,2304]{1,0:T(8,128)}, f32[768,768]{1,0:T(8,128)}, f32[768,2304]{1,0:T(8,128)}, f32[1152,768]{1,0:T(8,128)}, f32[768]{0:T(1024)}, /*index=5*/f32[768]{0:T(1024)}) custom-call(bf16[52,768,128]{2,1,0:T(8,128)(2,1)} %get-tuple-element.19.g, bf16[768,2304]{1,0:T(8,128)(2,1)} %wqkv.1, f32[768]{0:T(1024)} %gain1.1), custom_call_target="tpu_custom_call" | custom-call | tf_op jit(solution)/shard_map/widen/pallas_call | solution.py:712
  191.0 0.0 copy-done.1
  191.0 0.9 copy.20
  191.9 0.0 copy-done
  191.9 0.9 copy.21
Async XLA Ops:
  178.7 12.3 %copy-start.1 = (bf16[2,256,768]{2,1,0:T(8,128)(2,1)S(1)}, bf16[2,256,768]{2,1,0:T(8,128)(2,1)}, u32[]{:S(2)}) copy-start(bf16[2,256,768]{2,1,0:T(8,128)(2,1)} %get-tuple-element.34) | copy-start | bytes 2359300
  178.7 13.2 %copy-start = (bf16[2,256,768]{2,1,0:T(8,128)(2,1)S(1)}, bf16[2,256,768]{2,1,0:T(8,128)(2,1)}, u32[]{:S(2)}) copy-start(bf16[2,256,768]{2,1,0:T(8,128)(2,1)} %get-tuple-element.35) | copy-start | bytes 2359300

commit v3 on v2

--- a/solution.py
+++ b/solution.py
@@ -127,11 +127,12 @@
     pltpu.make_async_copy(ref, ref, sem).wait()
 
 
-LINK_RATE, CORE_RATE, ROUND_LATENCY = 44e3, 500e3, 2.5
+LINK_RATE, CORE_RATE, ROUND_LATENCY = 41e3, 460e3, 3.0
 STEP_TIME, ADD_TIME = 0.1, 0.4e-6
-PIECE_TIME = {"feed": 1.1, "mix": 1.8, "norm": 2.8, "wo": 1.5, "do": 2.0, "far": 1.25, "near": 1.25, "join": 1.8, "dx": 2.2}
+PIECE_TIME = {"feed": 1.1, "mix": 1.2, "norm": 5.0, "wo": 1.0, "do": 2.2, "far": 1.25, "near": 1.25, "join": 2.5, "dx": 4.0}
 FEED_GROUPS = ((0, 2), (2, 4), (4, 6), (6, 8))
 FIRST_PAIRS = 4
+ORDERS = "01001051010101010301054101"
 
 
 def log2(n):
@@ -160,10 +161,11 @@
 
 def axis_order(index, n_doc, n_seq):
     doc_axes, seq_axes = axes_of(n_doc, n_seq)
-    turn = (0, 1, 0, 0, 1, 1)[index % 6] * (len(doc_axes) // 2)
+    code = int(ORDERS[index % len(ORDERS)])
+    turn = code % 2 * (len(doc_axes) // 2)
     doc_axes = doc_axes[turn:] + doc_axes[:turn]
-    near, far = seq_axes[:-1], seq_axes[-1:]
-    return (near + doc_axes if index % 3 == 2 else doc_axes + near) + far
+    place = len(doc_axes) * (2 - code // 2) // 2
+    return doc_axes[:place] + seq_axes[:-1] + doc_axes[place:] + seq_axes[-1:]
 
 
 def stream_plan(width, ff):
@@ -175,20 +177,19 @@
         streams.append(Stream(first, second, count))
 
     for low, high in FEED_GROUPS:
-        count = (high - low) // 2
         for base in (0, ffs, 2 * ffs):
-            add(("feed", high - 1), base + low, base + low + count, count)
+            add(("feed", high - 1), base + low, base + low + 1, 1)
     covered = FEED_GROUPS[-1][1]
     assert ffs - covered == 1 and pairs % 2 == 0
     add(("feed", ffs - 1), covered, ffs + covered, 1)
     add(("norm", 0), 2 * ffs + covered, 3 * ffs + pairs, 1)
-    half = pairs // 2
-    add(("wo", 0), 3 * ffs, 3 * ffs + half, half)
+    for start in range(3 * ffs, 3 * ffs + pairs, 2):
+        add(("wo", 0), start, start + 1, 1)
     base = 3 * ffs + pairs + 1
     for part, (low, high) in enumerate(((0, FIRST_PAIRS), (FIRST_PAIRS, pairs))):
         for third in range(3):
-            start, count = base + third * pairs + low, (high - low) // 2
-            add(("join", part), start, start + count, count)
+            for start in range(base + third * pairs + low, base + third * pairs + high, 2):
+                add(("join", part), start, start + 1, 1)
     return streams, ready, base + 3 * pairs
 
 
@@ -222,7 +223,7 @@
         begin = max(when, free.get(axis, 0.0))
         free[axis] = begin + size / rate
         if axis == far:
-            free[near] = max(free.get(near, 0.0), begin) + 0.5 * size / LINK_RATE
+            free[near] = max(free.get(near, 0.0), begin) + size / LINK_RATE
         return free[axis]
 
     def depart(index, leg, when):
@@ -435,11 +436,12 @@
         return pl.ds(pl.multiple_of(base + j * LANES * count, LANES), LANES * count)
 
     for slot in range(2):
-        wait_bytes(xs.at[pl.ds(slot * rows, rows)], recv_sem.at[slot])
-    spread(cot_in, cs, 2, send_or_keep)
-
-    unit, _ = row_stats(xs[...].astype(F32))
-    xn[...] = (unit * gain1).astype(BF16)
+        here = pl.ds(slot * rows, rows)
+        wait_bytes(xs.at[here], recv_sem.at[slot])
+        if slot == 1:
+            spread(cot_in, cs, 2, send_or_keep)
+        unit, _ = row_stats(xs[here].astype(F32))
+        xn[here] = (unit * gain1).astype(BF16)
     for i in (0, 4, 5):
         loads[i].wait()
 
@@ -453,16 +455,21 @@
         v[:tokens, tile(j)] = both[:, LANES:].astype(BF16)
         return 0
 
-    lax.fori_loop(0, pairs, project, 0)
-    kv_copies = [
-        pltpu.make_async_remote_copy(
-            src_ref=ref.at[pl.ds(0, tokens)], dst_ref=ref.at[pl.ds(tokens, tokens)],
-            send_sem=kv_send.at[i], recv_sem=kv_recv.at[i], device_id=sibling, device_id_type=MESH,
-        )
-        for i, ref in enumerate((k, v))
-    ]
-    for copy in kv_copies:
-        copy.start()
+    def kv_copies(group):
+        lanes = tile(group, 0, pairs // 2)
+        return [
+            pltpu.make_async_remote_copy(
+                src_ref=ref.at[pl.ds(0, tokens), lanes], dst_ref=ref.at[pl.ds(tokens, tokens), lanes],
+                send_sem=kv_send.at[2 * i + group], recv_sem=kv_recv.at[2 * i + group],
+                device_id=sibling, device_id_type=MESH,
+            )
+            for i, ref in enumerate((k, v))
+        ]
+
+    for group in range(2):
+        lax.fori_loop(group * (pairs // 2), (group + 1) * (pairs // 2), project, 0)
+        for copy in kv_copies(group):
+            copy.start()
 
     def project_q(j, _):
         both = nn(xn[...], wqkv[:, tile(j, 0, 2)])
@@ -471,10 +478,8 @@
         return 0
 
     lax.fori_loop(0, pairs // 2, project_q, 0)
-    for copy in kv_copies:
-        copy.wait()
-
-    def attend(j, _):
+
+    def attend(j):
         lanes = tile(j)
         k2, vt, q2 = k[:, lanes], v[:, lanes].T, q[:, lanes]
         mixed = []
@@ -488,9 +493,15 @@
                 nn(vt[sub * HEAD_DIM : (sub + 1) * HEAD_DIM], weights.astype(BF16)) * (1.0 / total)
             )
         att[:, lanes] = jnp.concatenate(mixed, axis=0).T.astype(BF16)
+
+    def attend_group(group, _):
+        for copy in kv_copies(group):
+            copy.wait()
+        for j in range(pairs // 2):
+            attend(group * (pairs // 2) + j)
         return 0
 
-    lax.fori_loop(0, pairs, attend, 0)
+    lax.fori_loop(0, 2, attend_group, 0)
 
     loads[1].wait()
     h[...] = xs[...].astype(F32) + nn(att[...], wo[...])
@@ -603,7 +614,7 @@
         sends = [
             pltpu.make_async_remote_copy(
                 src_ref=away[i].at[:, lanes], dst_ref=landed.at[i, :, lanes],
-                send_sem=kv_send.at[2 + 2 * part + i], recv_sem=kv_recv.at[2 + 2 * part + i],
+                send_sem=kv_send.at[4 + 2 * part + i], recv_sem=kv_recv.at[4 + 2 * part + i],
                 device_id=sibling, device_id_type=MESH,
             )
             for i in range(2)
@@ -675,7 +686,7 @@
             pltpu.VMEM((total, width, LANES), BF16),
             pltpu.VMEM((slots, Reducer.landing_rows(width, rounds), LANES), BF16),
             pltpu.VMEM((slots, width, LANES), BF16),
-            dma((6,)), dma((8,)), dma((8,)), dma((6,)), dma((6,)),
+            dma((6,)), dma((8,)), dma((8,)), dma((8,)), dma((8,)),
             dma((len(streams), legs)), dma((len(streams), legs)), dma((len(streams),)),
         ],
         compiler_params=pltpu.CompilerParams(collective_id=0, has_side_effects=True, vmem_limit_bytes=VMEM_LIMIT),
@@ -683,7 +694,9 @@
     )(inputs, cotangent, gain1, gain2, wqkv, wo, win, wout, cos, sin)
 
 
-def widen_kernel(ff, width, g, wqkv, gain1, dqkv_o, dwo_o, dwin_o, dwout_o, gain1_o, gain2_o):
+def widen_kernel(ff, width, g, wqkv, gain1, out, dx, dqkv_o, dwo_o, dwin_o, dwout_o, gain1_o, gain2_o, out_o, dx_o):
+    out_o[...] = out[...]
+    dx_o[...] = dx[...]
     ffs, pairs = ff // LANES, width // LANES
     base = 3 * ffs + pairs + 1
     for j in range(ffs):
@@ -703,29 +716,31 @@
     gain1_o[...] = (total / gain1[...].reshape(1, LANES))[0]
 
 
-def widen(ff, g, wqkv, gain1):
+def widen(ff, g, wqkv, gain1, out, dx):
     total, width, _ = g.shape
     sds = jax.ShapeDtypeStruct
     across = lambda i: (i, 0)
     down = lambda i: (0, i)
     flat = pl.BlockSpec((LANES,), lambda i: (i,))
+    blocks, rows, _ = out.shape
+    token = pl.BlockSpec((blocks, rows, LANES), lambda i: (0, 0, i))
     return pl.pallas_call(
         functools.partial(widen_kernel, ff, width),
         grid=(width // LANES,),
         out_shape=[
             sds(wqkv.shape, F32), sds((width, width), F32), sds((width, 2 * ff), F32), sds((ff, width), F32),
-            sds((width,), F32), sds((width,), F32),
+            sds((width,), F32), sds((width,), F32), sds(out.shape, BF16), sds(dx.shape, BF16),
         ],
         in_specs=[
-            pl.BlockSpec((total, LANES, LANES), lambda i: (0, i, 0)), pl.BlockSpec((LANES, wqkv.shape[1]), across), flat,
+            pl.BlockSpec((total, LANES, LANES), lambda i: (0, i, 0)), pl.BlockSpec((LANES, wqkv.shape[1]), across), flat, token, token,
         ],
         out_specs=[
             pl.BlockSpec((LANES, wqkv.shape[1]), across), pl.BlockSpec((LANES, width), across),
-            pl.BlockSpec((LANES, 2 * ff), across), pl.BlockSpec((ff, LANES), down), flat, flat,
+            pl.BlockSpec((LANES, 2 * ff), across), pl.BlockSpec((ff, LANES), down), flat, flat, token, token,
         ],
         compiler_params=pltpu.CompilerParams(vmem_limit_bytes=VMEM_LIMIT),
         name="widen",
-    )(g, wqkv, gain1)
+    )(g, wqkv, gain1, out, dx)
 
 
 def rotary_tables(length):
@@ -750,7 +765,7 @@
         n_doc, n_seq, inputs, cotangent, attn_gain, mlp_gain,
         qkv_weight, attn_out_weight, mlp_in_weight, mlp_out_weight, cos, sin,
     )
-    dqkv, dwo, dwin, dwout, dgain1, dgain2 = widen(ff, grads, qkv_weight, attn_gain)
+    dqkv, dwo, dwin, dwout, dgain1, dgain2, output, dx = widen(ff, grads, qkv_weight, attn_gain, output, dx)
     return output, dx, dgain1, dqkv, dwo, dgain2, dwin, dwout
 
 

time: 193 us -> 175 us (0.907)
  Pallas kernels: 190 us -> 174 us
    pallas_call x1, Pallas kernels: 178 us -> 161 us  [layer(): pl.pallas_call(functools.partial(layer_kernel, n_doc, n_seq), out_shape=[...]
where the time goes in v3:
time: 175 us
  Pallas kernels  174 us (99%)
    pallas_call x1, Pallas kernels, layer(): pl.pallas_call(functools.partial(layer_kernel, n_doc, n_seq), out_shape=[...  161 us
    pallas_call x1, Pallas kernels, widen(): pl.pallas_call(functools.partial(widen_kernel, ff, width), grid=(width //...  13.1 us

profile of v3, /device:TPU:0, one launch (start us, length us, event | category | flops | bytes accessed | tf_op | source)
XLA Modules:
  0.0 175.2 jit_solution(2582369099780968020)
XLA Ops:
  0.6 161.2 %layer.1 = (bf16[2,256,768]{2,1,0:T(8,128)(2,1)}, bf16[2,256,768]{2,1,0:T(8,128)(2,1)}, bf16[52,768,128]{2,1,0:T(8,128)(2,1)}) custom-call(bf16[2,256,768]{2,1,0:T(8,128)(2,1)} %x_in.1, bf16[2,256,768]{2,1,0:T(8,128)(2,1)} %cot_in.1, f32[768]{0:T(1024)} %gain1.1, f32[768]{0:T(1024)} %gain2_in.1, bf16[768,2304]{1,0:T(8,128)(2,1)} %wqkv.1, ...), custom_call_target="tpu_custom_call" | custom-call | tf_op jit(solution)/shard_map/layer/pallas_call | solution.py:669
  161.9 13.1 %widen.1 = (f32[768,2304]{1,0:T(8,128)}, f32[768,768]{1,0:T(8,128)}, f32[768,2304]{1,0:T(8,128)}, f32[1152,768]{1,0:T(8,128)}, f32[768]{0:T(1024)}, /*index=5*/f...) custom-call(bf16[52,768,128]{2,1,0:T(8,128)(2,1)} %get-tuple-element.19.g, bf16[768,2304]{1,0:T(8,128)(2,1)} %wqkv.1, ...), custom_call_target="tpu_custom_call" | custom-call | tf_op jit(solution)/shard_map/widen/pallas_call | solution.py:727

commit v4 on v3

--- a/solution.py
+++ b/solution.py
@@ -86,14 +86,21 @@
 
 class Exchange:
     def __init__(self, doc, seq, n_seq):
+        assert n_seq == 4
         core = doc % 2
-        half = n_seq // 2
-        base = doc - core
-        self.out_targets = [(base + seq // half, 2 * core + block) for block in range(2)]
-        self.out_slot = seq % half
-        self.back_targets = [(base + seq // 2, half * core + slot) for slot in range(2)]
-        self.back_block = seq % 2
-        self.doc, self.seq = doc, seq
+        self.doc, self.seq, self.core = doc, seq, core
+        self.base = doc - core
+        side = seq // 2
+        self.near_first = [seq, flipped(seq, 1), 2 - side, 3 - 3 * side]
+        self.block_first = (1 - core) * side
+
+    def out_piece(self, n):
+        block = self.block_first + n // 2 - 2 * self.block_first * (n // 2)
+        half = n % 2
+        return block, half, (self.base + half, 2 * self.core + block)
+
+    def back_target(self, quarter):
+        return (self.base + self.seq // 2, quarter)
 
     def is_self(self, target):
         return jnp.logical_and(target[0] == self.doc, target[1] == self.seq)
@@ -127,12 +134,14 @@
     pltpu.make_async_copy(ref, ref, sem).wait()
 
 
-LINK_RATE, CORE_RATE, ROUND_LATENCY = 41e3, 460e3, 3.0
+LINK_RATE, CORE_RATE, ROUND_LATENCY = 42.3e3, 474e3, 3.0
 STEP_TIME, ADD_TIME = 0.1, 0.4e-6
 PIECE_TIME = {"feed": 1.1, "mix": 1.2, "norm": 5.0, "wo": 1.0, "do": 2.2, "far": 1.25, "near": 1.25, "join": 2.5, "dx": 4.0}
 FEED_GROUPS = ((0, 2), (2, 4), (4, 6), (6, 8))
 FIRST_PAIRS = 4
-ORDERS = "01001051010101010301054101"
+ORDERS = "10304211011410131011330222"
+OUT, DX = -1, -2
+OUT_AFTER, DX_GAP = (9, 9, 9, 12), 12.0
 
 
 def log2(n):
@@ -226,6 +235,10 @@
             free[near] = max(free.get(near, 0.0), begin) + size / LINK_RATE
         return free[axis]
 
+    def leave(chunk, when):
+        if chunk:
+            occupy(near if chunk == 1 else far, 196e3, when)
+
     def depart(index, leg, when):
         flying.append((occupy(*legs(index)[leg], when) + ROUND_LATENCY, index, leg))
 
@@ -242,18 +255,28 @@
     for piece in pieces:
         now += PIECE_TIME[piece[0]]
         actions = steps.setdefault(piece, [])
-        if piece[0] in ("mix", "dx"):
-            occupy(far, 393e3, now)
-            occupy(near, 200e3, now)
         for index in ready.get(piece, ()):
             actions.append((index, -1))
             depart(index, 0, now)
             now += STEP_TIME
+        for chunk, place in enumerate(OUT_AFTER):
+            if piece == pieces[place]:
+                actions.append((OUT, chunk))
+                leave(chunk, now)
+                now += STEP_TIME
         while flying and min(flying)[0] <= now:
             now, action = serve(now)
             actions.append(action)
     last = steps.setdefault("end", [])
-    while flying:
+    begin, chunk = now, 0
+    while flying or chunk < n_seq:
+        upcoming = max(now, min(flying)[0]) if flying else now
+        if chunk < n_seq and (not flying or upcoming >= begin + chunk * DX_GAP):
+            leave(chunk, now)
+            last.append((DX, chunk))
+            now += STEP_TIME
+            chunk += 1
+            continue
         now, action = serve(now)
         last.append(action)
     return steps
@@ -380,7 +403,7 @@
     doc, seq = lax.axis_index("doc"), lax.axis_index("seq")
     core = doc % 2
     ex = Exchange(doc, seq, n_seq)
-    rows = x_in.shape[1]
+    half = x_in.shape[1] // 2
     tokens, width = xs.shape
     ff = wout.shape[0]
     ffs, pairs = ff // LANES, width // LANES
@@ -390,27 +413,38 @@
         pltpu.make_async_copy(s, d, w_sem.at[i])
         for i, (s, d) in enumerate(
             [(wqkv_in, wqkv), (wo_in, wo), (win_in, win), (wout_in, wout)]
-            + [(t.at[pl.ds(core * tokens, tokens)], d) for t, d in ((cos_in, cos), (sin_in, sin))]
+            + [
+                (t.at[pl.ds((2 * quarter + core) * half, half)], d.at[pl.ds(quarter * half, half)])
+                for t, d in ((cos_in, cos), (sin_in, sin))
+                for quarter in range(n_seq)
+            ]
         )
     ]
+    loads[0].start()
+    for load in loads[4:]:
+        load.start()
     greet(group_partners(doc, seq, n_seq) + [(flipped(doc, w), seq) for _, w in axes_of(n_doc, n_seq)[0]])
 
+    def rows_of(slot):
+        return pl.ds(pl.multiple_of(slot * half, half), half)
+
     def spread(src, dst, base, act):
-        for block in range(2):
+        for n in range(n_seq):
+            block, part, target = ex.out_piece(n)
             act(
-                ex, ex.out_targets[block], src.at[block], dst.at[pl.ds(ex.out_slot * rows, rows)],
-                send_sem.at[base + block], recv_sem.at[base + ex.out_slot],
+                ex, target, src.at[block, pl.ds(part * half, half)], dst.at[rows_of(seq)],
+                send_sem.at[base + n], recv_sem.at[base + seq],
             )
 
-    def gather(src, dst, base, act):
-        for slot in range(2):
-            act(
-                ex, ex.back_targets[slot], src.at[pl.ds(slot * rows, rows)], dst.at[ex.back_block],
-                send_sem.at[base + slot], recv_sem.at[base + ex.back_block],
-            )
+    def gather(src, dst, base, n, act):
+        quarter = ex.near_first[n]
+        act(
+            ex, ex.back_target(quarter), src.at[rows_of(quarter)], dst.at[seq % 2, rows_of(core)],
+            send_sem.at[base + n], recv_sem.at[base + 2 * (seq % 2) + core],
+        )
 
     spread(x_in, xs, 0, send_or_keep)
-    for load in loads:
+    for load in loads[1:4]:
         load.start()
     gain1, gain2 = gain1_in[...].reshape(1, width), gain2_in[...].reshape(1, width)
 
@@ -419,8 +453,13 @@
     reducer = Reducer(streams, n_doc, n_seq, doc, seq, grads, landing, final, g_o, sum_send, sum_recv, own_sem)
 
     def after(piece):
-        for action in steps.get(piece, ()):
-            reducer.act(*action)
+        for index, leg in steps.get(piece, ()):
+            if index == OUT:
+                gather(outs, out_o, 8, leg, send_or_keep)
+            elif index == DX:
+                gather(do, dx_o, 12, leg, send_or_keep)
+            else:
+                reducer.act(index, leg)
 
     def loop(name, low, high, body):
         def one(j, _):
@@ -435,58 +474,59 @@
     def tile(j, base=0, count=1):
         return pl.ds(pl.multiple_of(base + j * LANES * count, LANES), LANES * count)
 
-    for slot in range(2):
-        here = pl.ds(slot * rows, rows)
-        wait_bytes(xs.at[here], recv_sem.at[slot])
-        if slot == 1:
-            spread(cot_in, cs, 2, send_or_keep)
-        unit, _ = row_stats(xs[here].astype(F32))
-        xn[here] = (unit * gain1).astype(BF16)
-    for i in (0, 4, 5):
-        loads[i].wait()
-
-    def roped(part, scale):
-        return ((part * cos[...] + turned(part) * sin[...]) * scale).astype(BF16)
-
-    def project(j, _):
-        weights = jnp.concatenate([wqkv[:, tile(j, width)], wqkv[:, tile(j, 2 * width)]], axis=1)
-        both = nn(xn[...], weights)
-        k[:tokens, tile(j)] = roped(both[:, :LANES], 1.0)
-        v[:tokens, tile(j)] = both[:, LANES:].astype(BF16)
-        return 0
-
-    def kv_copies(group):
-        lanes = tile(group, 0, pairs // 2)
+    def roped(part, here, scale):
+        return ((part * cos[here] + turned(part) * sin[here]) * scale).astype(BF16)
+
+    def kv_copies(n):
+        here = rows_of(ex.near_first[n])
+        there = pl.ds(pl.multiple_of(tokens + ex.near_first[n] * half, half), half)
         return [
             pltpu.make_async_remote_copy(
-                src_ref=ref.at[pl.ds(0, tokens), lanes], dst_ref=ref.at[pl.ds(tokens, tokens), lanes],
-                send_sem=kv_send.at[2 * i + group], recv_sem=kv_recv.at[2 * i + group],
-                device_id=sibling, device_id_type=MESH,
+                src_ref=ref.at[here], dst_ref=ref.at[there], send_sem=kv_send.at[2 * n + i],
+                recv_sem=kv_recv.at[2 * n + i], device_id=sibling, device_id_type=MESH,
             )
             for i, ref in enumerate((k, v))
         ]
 
-    for group in range(2):
-        lax.fori_loop(group * (pairs // 2), (group + 1) * (pairs // 2), project, 0)
-        for copy in kv_copies(group):
+    loads[0].wait()
+    for load in loads[4:]:
+        load.wait()
+    for n in range(n_seq):
+        here = rows_of(ex.near_first[n])
+        wait_bytes(xs.at[here], recv_sem.at[ex.near_first[n]])
+        if n == n_seq - 2:
+            spread(cot_in, cs, 4, send_or_keep)
+        unit, _ = row_stats(xs[here].astype(F32))
+        normed = (unit * gain1).astype(BF16)
+        xn[here] = normed
+
+        def project(j, _, here=here):
+            weights = jnp.concatenate([wqkv[:, tile(j, width)], wqkv[:, tile(j, 2 * width)]], axis=1)
+            both = nn(xn[here], weights)
+            k[here, tile(j)] = roped(both[:, :LANES], here, 1.0)
+            v[here, tile(j)] = both[:, LANES:].astype(BF16)
+            return 0
+
+        lax.fori_loop(0, pairs, project, 0)
+        for copy in kv_copies(n):
             copy.start()
 
-    def project_q(j, _):
-        both = nn(xn[...], wqkv[:, tile(j, 0, 2)])
-        for t in range(2):
-            q[:, tile(2 * j + t)] = roped(both[:, t * LANES : (t + 1) * LANES], 0.125)
-        return 0
-
-    lax.fori_loop(0, pairs // 2, project_q, 0)
+        def project_q(j, _, here=here):
+            both = nn(xn[here], wqkv[:, tile(j, 0, 2)])
+            for t in range(2):
+                q[here, tile(2 * j + t)] = roped(both[:, t * LANES : (t + 1) * LANES], here, 0.125)
+            return 0
+
+        lax.fori_loop(0, pairs // 2, project_q, 0)
 
     def attend(j):
         lanes = tile(j)
         k2, vt, q2 = k[:, lanes], v[:, lanes].T, q[:, lanes]
+        scores = [nt(one_head(k2, sub), q2) for sub in range(2)]
         mixed = []
         for sub in range(2):
-            scores = nt(one_head(k2, sub), q2)
-            top = jnp.max(scores, axis=0, keepdims=True)
-            weights = jnp.exp(scores - top)
+            top = jnp.max(scores[sub], axis=0, keepdims=True)
+            weights = jnp.exp(scores[sub] - top)
             total = jnp.sum(weights, axis=0, keepdims=True)
             lse[j, sub : sub + 1, :] = top + jnp.log(total)
             mixed.append(
@@ -495,12 +535,13 @@
         att[:, lanes] = jnp.concatenate(mixed, axis=0).T.astype(BF16)
 
     def attend_group(group, _):
-        for copy in kv_copies(group):
-            copy.wait()
         for j in range(pairs // 2):
             attend(group * (pairs // 2) + j)
         return 0
 
+    for n in range(n_seq):
+        for copy in kv_copies(n):
+            copy.wait()
     lax.fori_loop(0, 2, attend_group, 0)
 
     loads[1].wait()
@@ -510,8 +551,8 @@
     xn2t[...] = xn2[...].T
     loads[2].wait()
     loads[3].wait()
-    for slot in range(2):
-        wait_bytes(cs.at[pl.ds(slot * rows, rows)], recv_sem.at[2 + slot])
+    for slot in range(n_seq):
+        wait_bytes(cs.at[rows_of(slot)], recv_sem.at[4 + slot])
     dmt[...] = cs[...].T
 
     def feed(j):
@@ -534,7 +575,6 @@
     loop("feed", 0, ffs, feed)
 
     outs[...] = (h[...] + nn(hid[...], wout[...])).astype(BF16)
-    gather(outs, out_o, 4, send_or_keep)
     after(("mix", 0))
 
     acc[...] = nt(dgu[...], win[...])
@@ -614,7 +654,7 @@
         sends = [
             pltpu.make_async_remote_copy(
                 src_ref=away[i].at[:, lanes], dst_ref=landed.at[i, :, lanes],
-                send_sem=kv_send.at[4 + 2 * part + i], recv_sem=kv_recv.at[4 + 2 * part + i],
+                send_sem=kv_send.at[8 + 2 * part + i], recv_sem=kv_recv.at[8 + 2 * part + i],
                 device_id=sibling, device_id_type=MESH,
             )
             for i in range(2)
@@ -639,17 +679,17 @@
     grad1 = nt(dqkv[...], wqkv[...])
     unit, scale = row_stats(xs[...].astype(F32))
     dx[...] = (dh[...] + norm_back(grad1, unit, scale, gain1)).astype(BF16)
-    gather(dx, dx_o, 6, send_or_keep)
     after(("dx", 0))
     after("end")
 
     spread(x_in, xs, 0, wait_sent)
-    spread(cot_in, cs, 2, wait_sent)
-    gather(outs, out_o, 4, wait_sent)
-    gather(dx, dx_o, 6, wait_sent)
-    for block in range(2):
-        wait_bytes(out_o.at[block], recv_sem.at[4 + block])
-        wait_bytes(dx_o.at[block], recv_sem.at[6 + block])
+    spread(cot_in, cs, 4, wait_sent)
+    for src, dst, base in ((outs, out_o, 8), (dx, dx_o, 12)):
+        for n in range(n_seq):
+            gather(src, dst, base, n, wait_sent)
+        for block in range(2):
+            for part in range(2):
+                wait_bytes(dst.at[block, pl.ds(part * half, half)], recv_sem.at[base + 2 * block + part])
 
 
 def layer(n_doc, n_seq, inputs, cotangent, gain1, gain2, wqkv, wo, win, wout, cos, sin):
@@ -686,7 +726,7 @@
             pltpu.VMEM((total, width, LANES), BF16),
             pltpu.VMEM((slots, Reducer.landing_rows(width, rounds), LANES), BF16),
             pltpu.VMEM((slots, width, LANES), BF16),
-            dma((6,)), dma((8,)), dma((8,)), dma((8,)), dma((8,)),
+            dma((12,)), dma((16,)), dma((16,)), dma((12,)), dma((12,)),
             dma((len(streams), legs)), dma((len(streams), legs)), dma((len(streams),)),
         ],
         compiler_params=pltpu.CompilerParams(collective_id=0, has_side_effects=True, vmem_limit_bytes=VMEM_LIMIT),

time: 175 us -> 172 us (0.983)
  Pallas kernels: 174 us -> 171 us
    pallas_call x1, Pallas kernels: 161 us -> 158 us  [layer(): pl.pallas_call(functools.partial(layer_kernel, n_doc, n_seq), out_shape=[...]
where the time goes in v4:
time: 172 us
  Pallas kernels  171 us (99%)
    pallas_call x1, Pallas kernels, layer(): pl.pallas_call(functools.partial(layer_kernel, n_doc, n_seq), out_shape=[...  158 us
    pallas_call x1, Pallas kernels, widen(): pl.pallas_call(functools.partial(widen_kernel, ff, width), grid=(width //...  13.1 us

profile of v4, /device:TPU:0, one launch (start us, length us, event | category | flops | bytes accessed | tf_op | source)
XLA Modules:
  0.0 172.2 jit_solution(8047254483479306923)
XLA Ops:
  0.6 158.3 %layer.1 = (bf16[2,256,768]{2,1,0:T(8,128)(2,1)}, bf16[2,256,768]{2,1,0:T(8,128)(2,1)}, bf16[52,768,128]{2,1,0:T(8,128)(2,1)}) custom-call(bf16[2,256,768]{2,1,0:T(8,128)(2,1)} %x_in.1, bf16[2,256,768]{2,1,0:T(8,128)(2,1)} %cot_in.1, f32[768]{0:T(1024)} %gain1.1, f32[768]{0:T(1024)} %gain2_in.1, bf16[768,2304]{1,0:T(8,128)(2,1)} %wqkv.1, ...), custom_call_target="tpu_custom_call" | custom-call | tf_op jit(solution)/shard_map/layer/pallas_call | solution.py:709
  158.9 13.1 %widen.1 = (f32[768,2304]{1,0:T(8,128)}, f32[768,768]{1,0:T(8,128)}, f32[768,2304]{1,0:T(8,128)}, f32[1152,768]{1,0:T(8,128)}, f32[768]{0:T(1024)}, /*index=5*/f...) custom-call(bf16[52,768,128]{2,1,0:T(8,128)(2,1)} %get-tuple-element.19.g, bf16[768,2304]{1,0:T(8,128)(2,1)} %wqkv.1, ...), custom_call_target="tpu_custom_call" | custom-call | tf_op jit(solution)/shard_map/widen/pallas_call | solution.py:767

commit v5 on v4

--- a/solution.py
+++ b/solution.py
@@ -134,14 +134,13 @@
     pltpu.make_async_copy(ref, ref, sem).wait()
 
 
-LINK_RATE, CORE_RATE, ROUND_LATENCY = 42.3e3, 474e3, 3.0
+LINK_RATE, CORE_RATE, ROUND_LATENCY, SPARE = 43225.0, 484500.0, 2.6, 1.0
 STEP_TIME, ADD_TIME = 0.1, 0.4e-6
-PIECE_TIME = {"feed": 1.1, "mix": 1.2, "norm": 5.0, "wo": 1.0, "do": 2.2, "far": 1.25, "near": 1.25, "join": 2.5, "dx": 4.0}
-FEED_GROUPS = ((0, 2), (2, 4), (4, 6), (6, 8))
+PIECE_TIME = {"feed": 2.0, "last": 1.1, "mix": 1.2, "norm": 3.5, "wo": 1.0, "do": 1.4, "far": 1.25, "near": 1.25, "join": 2.5, "dx": 4.0}
 FIRST_PAIRS = 4
-ORDERS = "10304211011410131011330222"
+ORDERS = "01"
 OUT, DX = -1, -2
-OUT_AFTER, DX_GAP = (9, 9, 9, 12), 12.0
+OUT_AFTER, DX_GAP = (5, 5, 6, 12), 12.0
 
 
 def log2(n):
@@ -185,12 +184,12 @@
         ready.setdefault(piece, []).append(len(streams))
         streams.append(Stream(first, second, count))
 
-    for low, high in FEED_GROUPS:
+    assert ffs % 2 == 1 and pairs % 2 == 0
+    covered = ffs - 1
+    for low in range(0, covered, 2):
         for base in (0, ffs, 2 * ffs):
-            add(("feed", high - 1), base + low, base + low + 1, 1)
-    covered = FEED_GROUPS[-1][1]
-    assert ffs - covered == 1 and pairs % 2 == 0
-    add(("feed", ffs - 1), covered, ffs + covered, 1)
+            add(("feed", low // 2), base + low, base + low + 1, 1)
+    add(("last", 0), covered, ffs + covered, 1)
     add(("norm", 0), 2 * ffs + covered, 3 * ffs + pairs, 1)
     for start in range(3 * ffs, 3 * ffs + pairs, 2):
         add(("wo", 0), start, start + 1, 1)
@@ -204,7 +203,7 @@
 
 def piece_list(ff, pairs):
     ffs = ff // LANES
-    pieces = [("feed", j) for j in range(ffs)]
+    pieces = [("feed", j) for j in range(ffs // 2)] + [("last", 0)]
     pieces += [("mix", 0), ("norm", 0), ("wo", 0), ("do", 0)]
     for part, (low, high) in enumerate(((0, FIRST_PAIRS), (FIRST_PAIRS, pairs))):
         pieces += [("far", j) for j in range(low, high)] + [("near", j) for j in range(low, high)]
@@ -264,7 +263,7 @@
                 actions.append((OUT, chunk))
                 leave(chunk, now)
                 now += STEP_TIME
-        while flying and min(flying)[0] <= now:
+        while flying and min(flying)[0] + SPARE <= now:
             now, action = serve(now)
             actions.append(action)
     last = steps.setdefault("end", [])
@@ -286,6 +285,7 @@
     def __init__(self, streams, n_doc, n_seq, doc, seq, grads, landing, final, out, send_sem, recv_sem, own_sem):
         self.streams, self.grads, self.landing, self.final, self.out = streams, grads, landing, final, out
         self.send_sem, self.recv_sem, self.own_sem = send_sem, recv_sem, own_sem
+        self.busy, self.unsent = False, []
         self.core = doc % 2
         self.rows = grads.shape[1]
         self.rounds = log2(n_doc) - 1 + log2(n_seq)
@@ -378,9 +378,17 @@
 
         lax.fori_loop(0, keep // block, body, 0)
 
+    def settle(self):
+        self.busy = False
+        for index, leg in self.unsent:
+            self.copy(index, leg).wait_send()
+
     def act(self, index, leg):
         if leg >= 0:
-            self.copy(index, leg).wait_send()
+            if self.busy:
+                self.unsent.append((index, leg))
+            else:
+                self.copy(index, leg).wait_send()
             self.copy(index, leg, True).wait_recv()
             if leg <= self.rounds:
                 self.add(index, leg)
@@ -397,7 +405,7 @@
     x_in, cot_in, gain1_in, gain2_in, wqkv_in, wo_in, win_in, wout_in, cos_in, sin_in,
     out_o, dx_o, g_o,
     xs, cs, outs, wqkv, wo, win, wout, cos, sin, xn, q, k, v, att, h, xn2, xn2t, hid, dgu, dmt, do, dh, acc, lse, dd,
-    dqt, landed, grads, landing, final,
+    dqt, landed, grads, landing, final, rms,
     w_sem, send_sem, recv_sem, kv_send, kv_recv, sum_send, sum_recv, own_sem,
 ):
     doc, seq = lax.axis_index("doc"), lax.axis_index("seq")
@@ -546,7 +554,9 @@
 
     loads[1].wait()
     h[...] = xs[...].astype(F32) + nn(att[...], wo[...])
-    unit2, _ = row_stats(h[...])
+    unit2, scale2 = row_stats(h[...])
+    dh[...] = unit2
+    rms[...] = scale2
     xn2[...] = (unit2 * gain2).astype(BF16)
     xn2t[...] = xn2[...].T
     loads[2].wait()
@@ -555,34 +565,38 @@
         wait_bytes(cs.at[rows_of(slot)], recv_sem.at[4 + slot])
     dmt[...] = cs[...].T
 
-    def feed(j):
-        both = nn(xn2[...], jnp.concatenate([win[:, tile(j)], win[:, tile(j, ff)]], axis=1))
-        gate, up = both[:, :LANES], both[:, LANES:]
+    def feed(j, count):
+        first = 2 * j
+        wide = count * LANES
+        lanes = pl.ds(pl.multiple_of(first * LANES, LANES), wide)
+        up_lanes = pl.ds(pl.multiple_of(ff + first * LANES, LANES), wide)
+        gate, up = nn(xn2[...], win[:, lanes]), nn(xn2[...], win[:, up_lanes])
         phi = 0.5 * (1.0 + lax.erf(gate * 0.7071067811865476))
         slope = phi + gate * (0.3989422804014327 * jnp.exp(-0.5 * gate * gate))
         active = gate * phi
         inner = (active * up).astype(BF16)
-        hid[:, tile(j)] = inner
-        dhid = nt(cs[...], wout[tile(j), :])
+        hid[:, lanes] = inner
+        dhid = nt(cs[...], wout[lanes, :])
         dgate, dup = (dhid * up * slope).astype(BF16), (dhid * active).astype(BF16)
-        dgu[:, tile(j)] = dgate
-        dgu[:, tile(j, ff)] = dup
-        grads[j] = nn(dmt[...], inner).astype(BF16)
-        pair = nn(xn2t[...], jnp.concatenate([dgate, dup], axis=1)).astype(BF16)
-        grads[ffs + j] = pair[:, :LANES]
-        grads[2 * ffs + j] = pair[:, LANES:]
-
-    loop("feed", 0, ffs, feed)
+        dgu[:, lanes] = dgate
+        dgu[:, up_lanes] = dup
+        for base, left, right in ((0, dmt, inner), (ffs, xn2t, dgate), (2 * ffs, xn2t, dup)):
+            part = nn(left[...], right).astype(BF16)
+            for t in range(count):
+                grads[base + first + t] = part[:, t * LANES : (t + 1) * LANES]
+
+    loop("feed", 0, ffs // 2, lambda j: feed(j, 2))
+    feed(ffs // 2, 1)
+    after(("last", 0))
 
     outs[...] = (h[...] + nn(hid[...], wout[...])).astype(BF16)
     after(("mix", 0))
 
     acc[...] = nt(dgu[...], win[...])
-    unit2, scale2 = row_stats(h[...])
-    grad2 = acc[...]
-    dh[...] = cs[...].astype(F32) + norm_back(grad2, unit2, scale2, gain2)
-    gain_terms = (grad2 * unit2).astype(BF16).T
-    grads[3 * ffs + pairs] = nn(gain_terms, jnp.ones((tokens, LANES), BF16)).astype(BF16)
+    unit2, grad2 = dh[...], acc[...]
+    gain_terms = jnp.sum(grad2 * unit2, axis=0, keepdims=True)
+    grads[3 * ffs + pairs] = jnp.broadcast_to(gain_terms, (LANES, width)).T.astype(BF16)
+    dh[...] = cs[...].astype(F32) + norm_back(grad2, unit2, rms[...], gain2)
     after(("norm", 0))
 
     datt = dh[...].astype(BF16)
@@ -594,17 +608,14 @@
     after(("wo", 0))
 
     do[...] = nt(datt, wo[...]).astype(BF16)
-    lane = lax.broadcasted_iota(jnp.int32, (8, LANES), 1)
-    row = lax.broadcasted_iota(jnp.int32, (8, LANES), 0)
-    pick = jnp.where(lane // HEAD_DIM == row, 1.0, 0.0).astype(F32)
+    lane = lax.broadcasted_iota(jnp.int32, (16, width), 1)
+    row = lax.broadcasted_iota(jnp.int32, (16, width), 0)
+    pick = jnp.where(lane // HEAD_DIM == row, 1.0, 0.0).astype(BF16)
+    product = do[...].astype(F32) * att[...].astype(F32)
+    high = product.astype(BF16)
+    sums = nt(pick, high) + nt(pick, (product - high.astype(F32)).astype(BF16))
     for j in range(pairs):
-        lanes = slice(j * LANES, (j + 1) * LANES)
-        product = do[:, lanes].astype(F32) * att[:, lanes].astype(F32)
-        sums = lax.dot_general(
-            pick, product, (((1,), (1,)), ((), ())),
-            precision=lax.Precision.HIGHEST, preferred_element_type=F32,
-        )
-        dd[j] = sums[:2]
+        dd[j] = sums[2 * j : 2 * j + 2]
     after(("do", 0))
 
     dqkv, xnt, dx = win.at[pl.ds(0, tokens)], xn2t, do
@@ -680,6 +691,7 @@
     unit, scale = row_stats(xs[...].astype(F32))
     dx[...] = (dh[...] + norm_back(grad1, unit, scale, gain1)).astype(BF16)
     after(("dx", 0))
+    reducer.settle()
     after("end")
 
     spread(x_in, xs, 0, wait_sent)
@@ -725,7 +737,7 @@
             pltpu.VMEM((pairs, LANES, tokens), F32), pltpu.VMEM((2, tokens, width), BF16),
             pltpu.VMEM((total, width, LANES), BF16),
             pltpu.VMEM((slots, Reducer.landing_rows(width, rounds), LANES), BF16),
-            pltpu.VMEM((slots, width, LANES), BF16),
+            pltpu.VMEM((slots, width, LANES), BF16), pltpu.VMEM((tokens, 1), F32),
             dma((12,)), dma((16,)), dma((16,)), dma((12,)), dma((12,)),
             dma((len(streams), legs)), dma((len(streams), legs)), dma((len(streams),)),
         ],

time: 172 us -> 163 us (0.948)
  Pallas kernels: 171 us -> 162 us
    pallas_call x1, Pallas kernels: 158 us -> 148 us  [layer(): pl.pallas_call(functools.partial(layer_kernel, n_doc, n_seq), out_shape=[...]
where the time goes in v5:
time: 163 us; the launch traced here: 162 us
  Pallas kernels  162 us (99%)
    pallas_call x1, Pallas kernels, layer(): pl.pallas_call(functools.partial(layer_kernel, n_doc, n_seq), out_shape=[...  148 us
    pallas_call x1, Pallas kernels, widen(): pl.pallas_call(functools.partial(widen_kernel, ff, width), grid=(width //...  13.1 us

profile of v5, /device:TPU:0, one launch (start us, length us, event | category | flops | bytes accessed | tf_op | source)
XLA Modules:
  0.0 162.4 jit_solution(5876994009360553352)
XLA Ops:
  0.6 148.4 %layer.1 = (bf16[2,256,768]{2,1,0:T(8,128)(2,1)}, bf16[2,256,768]{2,1,0:T(8,128)(2,1)}, bf16[52,768,128]{2,1,0:T(8,128)(2,1)}) custom-call(bf16[2,256,768]{2,1,0:T(8,128)(2,1)} %x_in.1, bf16[2,256,768]{2,1,0:T(8,128)(2,1)} %cot_in.1, f32[768]{0:T(1024)} %gain1.1, f32[768]{0:T(1024)} %gain2_in.1, bf16[768,2304]{1,0:T(8,128)(2,1)} %wqkv.1, ...), custom_call_target="tpu_custom_call" | custom-call | tf_op jit(solution)/shard_map/layer/pallas_call | solution.py:721
  149.1 13.1 %widen.1 = (f32[768,2304]{1,0:T(8,128)}, f32[768,768]{1,0:T(8,128)}, f32[768,2304]{1,0:T(8,128)}, f32[1152,768]{1,0:T(8,128)}, f32[768]{0:T(1024)}, /*index=5*/f...) custom-call(bf16[52,768,128]{2,1,0:T(8,128)(2,1)} %get-tuple-element.19.g, bf16[768,2304]{1,0:T(8,128)(2,1)} %wqkv.1, ...), custom_call_target="tpu_custom_call" | custom-call | tf_op jit(solution)/shard_map/widen/pallas_call | solution.py:779

commit v6 on v5

--- a/solution.py
+++ b/solution.py
@@ -134,13 +134,14 @@
     pltpu.make_async_copy(ref, ref, sem).wait()
 
 
-LINK_RATE, CORE_RATE, ROUND_LATENCY, SPARE = 43225.0, 484500.0, 2.6, 1.0
+LINK_RATE, CORE_RATE, ROUND_LATENCY, SPARE = 44135.0, 510e3, 2.6, 1.5
+NEAR_SHARE, FAR_SHARE = 1.0, 0.25
 STEP_TIME, ADD_TIME = 0.1, 0.4e-6
 PIECE_TIME = {"feed": 2.0, "last": 1.1, "mix": 1.2, "norm": 3.5, "wo": 1.0, "do": 1.4, "far": 1.25, "near": 1.25, "join": 2.5, "dx": 4.0}
 FIRST_PAIRS = 4
-ORDERS = "01"
+ORDERS = "11000110001010111001101100"
 OUT, DX = -1, -2
-OUT_AFTER, DX_GAP = (5, 5, 6, 12), 12.0
+OUT_AFTER, DX_GAP = (5, 5, 5, 8), 14.0
 
 
 def log2(n):
@@ -230,8 +231,9 @@
         rate = CORE_RATE if axis == "core" else LINK_RATE / 2 if axis == far else LINK_RATE
         begin = max(when, free.get(axis, 0.0))
         free[axis] = begin + size / rate
-        if axis == far:
-            free[near] = max(free.get(near, 0.0), begin) + size / LINK_RATE
+        for axis_from, axis_to, share, speed in ((far, near, NEAR_SHARE, LINK_RATE), (near, far, FAR_SHARE, LINK_RATE / 2)):
+            if axis == axis_from and share:
+                free[axis_to] = max(free.get(axis_to, 0.0), begin) + share * size / speed
         return free[axis]
 
     def leave(chunk, when):

time: 163 us -> 160 us (0.982)
  Pallas kernels: 162 us -> 159 us
    pallas_call x1, Pallas kernels: 148 us -> 146 us  [layer(): pl.pallas_call(functools.partial(layer_kernel, n_doc, n_seq), out_shape=[...]
where the time goes in v6:
time: 160 us
  Pallas kernels  159 us (99%)
    pallas_call x1, Pallas kernels, layer(): pl.pallas_call(functools.partial(layer_kernel, n_doc, n_seq), out_shape=[...  146 us
    pallas_call x1, Pallas kernels, widen(): pl.pallas_call(functools.partial(widen_kernel, ff, width), grid=(width //...  13.1 us

profile of v6, /device:TPU:0, one launch (start us, length us, event | category | flops | bytes accessed | tf_op | source)
XLA Modules:
  0.0 160.0 jit_solution(7411947839985548983)
XLA Ops:
  0.6 146.1 %layer.1 = (bf16[2,256,768]{2,1,0:T(8,128)(2,1)}, bf16[2,256,768]{2,1,0:T(8,128)(2,1)}, bf16[52,768,128]{2,1,0:T(8,128)(2,1)}) custom-call(bf16[2,256,768]{2,1,0:T(8,128)(2,1)} %x_in.1, bf16[2,256,768]{2,1,0:T(8,128)(2,1)} %cot_in.1, f32[768]{0:T(1024)} %gain1.1, f32[768]{0:T(1024)} %gain2_in.1, bf16[768,2304]{1,0:T(8,128)(2,1)} %wqkv.1, ...), custom_call_target="tpu_custom_call" | custom-call | tf_op jit(solution)/shard_map/layer/pallas_call | solution.py:723
  146.7 13.1 %widen.1 = (f32[768,2304]{1,0:T(8,128)}, f32[768,768]{1,0:T(8,128)}, f32[768,2304]{1,0:T(8,128)}, f32[1152,768]{1,0:T(8,128)}, f32[768]{0:T(1024)}, /*index=5*/f...) custom-call(bf16[52,768,128]{2,1,0:T(8,128)(2,1)} %get-tuple-element.19.g, bf16[768,2304]{1,0:T(8,128)(2,1)} %wqkv.1, ...), custom_call_target="tpu_custom_call" | custom-call | tf_op jit(solution)/shard_map/widen/pallas_call | solution.py:781

commit v7 on v6

--- a/solution.py
+++ b/solution.py
@@ -205,7 +205,7 @@
 def piece_list(ff, pairs):
     ffs = ff // LANES
     pieces = [("feed", j) for j in range(ffs // 2)] + [("last", 0)]
-    pieces += [("mix", 0), ("norm", 0), ("wo", 0), ("do", 0)]
+    pieces += [("mix", 0), ("norm", 0), ("do", 0), ("wo", 0)]
     for part, (low, high) in enumerate(((0, FIRST_PAIRS), (FIRST_PAIRS, pairs))):
         pieces += [("far", j) for j in range(low, high)] + [("near", j) for j in range(low, high)]
         pieces.append(("join", part))
@@ -602,13 +602,6 @@
     after(("norm", 0))
 
     datt = dh[...].astype(BF16)
-    att_t = att[...].T
-    for j in range(pairs // 2):
-        both = nn(att_t, datt[:, 2 * j * LANES : (2 * j + 2) * LANES]).astype(BF16)
-        for t in range(2):
-            grads[3 * ffs + 2 * j + t] = both[:, t * LANES : (t + 1) * LANES]
-    after(("wo", 0))
-
     do[...] = nt(datt, wo[...]).astype(BF16)
     lane = lax.broadcasted_iota(jnp.int32, (16, width), 1)
     row = lax.broadcasted_iota(jnp.int32, (16, width), 0)
@@ -619,6 +612,13 @@
     for j in range(pairs):
         dd[j] = sums[2 * j : 2 * j + 2]
     after(("do", 0))
+
+    att_t = att[...].T
+    for j in range(pairs // 2):
+        both = nn(att_t, datt[:, 2 * j * LANES : (2 * j + 2) * LANES]).astype(BF16)
+        for t in range(2):
+            grads[3 * ffs + 2 * j + t] = both[:, t * LANES : (t + 1) * LANES]
+    after(("wo", 0))
 
     dqkv, xnt, dx = win.at[pl.ds(0, tokens)], xn2t, do
     away, own = (xn2, att), (h, acc)

time: 160 us -> 160 us (level)
  no operation moved by 1% of the time
where the time goes in v7:
time: 160 us; the launch traced here: 159 us
  Pallas kernels  159 us (99%)
    pallas_call x1, Pallas kernels, layer(): pl.pallas_call(functools.partial(layer_kernel, n_doc, n_seq), out_shape=[...  145 us
    pallas_call x1, Pallas kernels, widen(): pl.pallas_call(functools.partial(widen_kernel, ff, width), grid=(width //...  13.1 us

profile of v7, /device:TPU:0, one launch (start us, length us, event | category | flops | bytes accessed | tf_op | source)
XLA Modules:
  0.0 159.4 jit_solution(3227728273296272797)
XLA Ops:
  0.6 145.5 %layer.1 = (bf16[2,256,768]{2,1,0:T(8,128)(2,1)}, bf16[2,256,768]{2,1,0:T(8,128)(2,1)}, bf16[52,768,128]{2,1,0:T(8,128)(2,1)}) custom-call(bf16[2,256,768]{2,1,0:T(8,128)(2,1)} %x_in.1, bf16[2,256,768]{2,1,0:T(8,128)(2,1)} %cot_in.1, f32[768]{0:T(1024)} %gain1.1, f32[768]{0:T(1024)} %gain2_in.1, bf16[768,2304]{1,0:T(8,128)(2,1)} %wqkv.1, ...), custom_call_target="tpu_custom_call" | custom-call | tf_op jit(solution)/shard_map/layer/pallas_call | solution.py:723
  146.1 13.1 %widen.1 = (f32[768,2304]{1,0:T(8,128)}, f32[768,768]{1,0:T(8,128)}, f32[768,2304]{1,0:T(8,128)}, f32[1152,768]{1,0:T(8,128)}, f32[768]{0:T(1024)}, /*index=5*/f...) custom-call(bf16[52,768,128]{2,1,0:T(8,128)(2,1)} %get-tuple-element.19.g, bf16[768,2304]{1,0:T(8,128)(2,1)} %wqkv.1, ...), custom_call_target="tpu_custom_call" | custom-call | tf_op jit(solution)/shard_map/widen/pallas_call | solution.py:781
